TPU v7x, 32 devices: a whole 2x2x4 slice. The times are simulated.
32 devices in a mesh: parts: 2 (over y), ha: 4 (over x, core), wa: 4 (over z).
Axes of the slice: x: 2, y: 2, z: 4, core: 2. Of those that a mesh axis runs over, the one named last changes fastest.
Arguments:
- token_ids: int32 [64, 64], P(('parts', 'ha', 'wa')), parts along dimension 0, may hold values from 0 to 63999
- neighbour_lists: int32 [8, 8, 6], P(('parts', 'ha'), 'wa'), parts along dimension 0, may hold values from 0 to 8, as said below
- codebook: bfloat16 [39, 512], replicated, may hold values from -10 to 10
- qkv_weight: bfloat16 [2, 512, 1536], replicated, may hold values from -0.25 to 0.25
- out_weight: bfloat16 [2, 512, 512], replicated, may hold values from -0.25 to 0.25
- logit_scale: float32 [2, 8], replicated, may hold values from 1 to 32
- conv_weight: bfloat16 [3, 3, 512, 256], replicated, may hold values from -0.09375 to 0.09375
Outputs:
- decoded: bfloat16 [64, 64, 256], P(('parts', 'ha'), 'wa'), parts along dimension 0
There are 2 independent parts, one for each index of `parts`. A program takes and returns all parts, laid end to end along the dimension named above; an argument that names none is the same for every part. Nothing has to cross between parts.
Inputs may be any that keep to these rules, and one draw needn't show every extreme that they name: `neighbour_lists`: each list holds 6 distinct neighbour numbers; the first is always 4, the block itself.
All inputs are finite; a program needn't handle non-finite values.
Results may differ from a plain program's by a relative error of at most 0.017.
Values may be sent and summed in bfloat16 or wider, within the bound.
No kernel may reach another device: no remote copies, remote signals or barrier semaphores. Data moves between devices by JAX's collectives and lax.ppermute only.
A program may use at most 64 MiB of HBM per device.

v0:
```python
import math

import jax
import jax.numpy as jnp
from jax import lax
from jax.sharding import PartitionSpec as P

D = 512
HEADS = 8
TILE = 8
NSEL = 6
BLOCKS = 2


digit_levels = (8, 8, 8, 5, 5, 5)
norm_eps = 1e-06


def with_halo(array, sides, width):
    for axis, dim in sides:
        size, length = (lax.axis_size(axis), array.shape[dim])
        up = [(i, (i + 1) % size) for i in range(size - 1)]
        down = [(j, i) for i, j in up]
        last = lax.slice_in_dim(array, length - width, length, axis=dim)
        initial = lax.slice_in_dim(array, 0, width, axis=dim)
        before = lax.ppermute(last, axis, up)
        after = lax.ppermute(initial, axis, down)
        array = jnp.concatenate([before, array, after], axis=dim)
    return array


def digit_slots(token_ids):
    result = []
    stride = 1
    for position in range(len(digit_levels) - 1, -1, -1):
        level_size = digit_levels[position]
        offset = sum(digit_levels[:position])
        result.append(offset + token_ids // stride % level_size)
        stride = stride * level_size
    return result


def normalize(values):
    wide32 = values.astype(jnp.float32)
    return wide32 * lax.rsqrt(jnp.mean(wide32 * wide32, axis=-1, keepdims=True) + norm_eps)


def head_norm(values):
    shaped = values.reshape(values.shape[:-1] + (HEADS, D // HEADS))
    return normalize(shaped).reshape(values.shape).astype(jnp.bfloat16)


def embed_ids(id_grid, codebook):
    flat_ids = id_grid.reshape(-1)
    slot_range = jnp.arange(codebook.shape[0], dtype=jnp.int32)[:, None]
    hits = jnp.zeros((codebook.shape[0], flat_ids.shape[0]), jnp.float32)
    for table_row in digit_slots(flat_ids):
        hits = hits + (slot_range == table_row[None, :]).astype(jnp.float32)
    embedded = lax.dot_general(
        hits.astype(jnp.bfloat16),
        codebook,
        (((0,), (0,)), ((), ())),
        preferred_element_type=jnp.float32,
    )
    return embedded.astype(jnp.bfloat16).reshape(id_grid.shape + (codebook.shape[1],))


def make_queries(normed, weight_block):
    return head_norm(jnp.dot(normed, weight_block[:, :D], preferred_element_type=jnp.float32))


def make_pairs(normed, weight_block):
    combined = jnp.dot(normed, weight_block[:, D:], preferred_element_type=jnp.float32)
    return jnp.concatenate(
        [head_norm(combined[..., :D]), combined[..., D:].astype(jnp.bfloat16)], axis=-1
    )


def attend(queries, pair_region, key_index, key_valid, factor):
    head_size = D // HEADS
    area = TILE * TILE
    query_rows = queries.shape[0] // TILE
    query_cols = queries.shape[1] // TILE
    count = query_rows * query_cols
    query_tiles = (
        queries.reshape(query_rows, TILE, query_cols, TILE, HEADS, head_size)
        .transpose(0, 2, 1, 3, 4, 5)
        .reshape(count, area, HEADS, head_size)
    )
    region_tiles = (
        pair_region.reshape(query_rows + 2, TILE, query_cols + 2, TILE, 2 * D)
        .transpose(0, 2, 1, 3, 4)
        .reshape((query_rows + 2) * (query_cols + 2), area, 2 * D)
    )
    gathered = jnp.take(region_tiles, key_index, axis=0).reshape(
        count, NSEL * area, 2, HEADS, head_size
    )
    allowed = jnp.take(key_valid, key_index, axis=0).reshape(count, NSEL * area)
    scores = (
        jnp.einsum(
            "tqhd,tkhd->thqk", query_tiles, gathered[:, :, 0], preferred_element_type=jnp.float32
        )
        * factor[None, :, None, None]
    )
    scores = jnp.where(allowed[:, None, None, :], scores, -1e30)
    peak = jnp.max(scores, axis=-1, keepdims=True)
    expo = jnp.exp(scores - peak)
    soft = (expo / jnp.sum(expo, axis=-1, keepdims=True)).astype(jnp.bfloat16)
    mixed = jnp.einsum(
        "thqk,tkhd->tqhd", soft, gathered[:, :, 1], preferred_element_type=jnp.float32
    ).astype(jnp.bfloat16)
    mixed = mixed.reshape(query_rows, query_cols, TILE, TILE, D).transpose(0, 2, 1, 3, 4)
    return mixed.reshape(query_rows * TILE, query_cols * TILE, D)


def attention_block(hidden, widened, key_index, key_valid, weight_block, out_block, scale_row):
    factor = scale_row / math.sqrt(D // HEADS)
    normed = normalize(hidden).astype(jnp.bfloat16)
    queries = make_queries(normed, weight_block)
    if widened is not None:
        pair_region = make_pairs(normalize(widened).astype(jnp.bfloat16), weight_block)
    else:
        pair_region = with_halo(make_pairs(normed, weight_block), (("ha", 0), ("wa", 1)), TILE)
    attended = attend(queries, pair_region, key_index, key_valid, factor)
    return (
        hidden.astype(jnp.float32)
        + jnp.dot(attended, out_block, preferred_element_type=jnp.float32)
    ).astype(jnp.bfloat16)


def local(token_ids, neighbour_lists, codebook, qkv_weight, out_weight, logit_scale, conv_weight):
    across = lax.axis_size("wa")
    downward = lax.axis_size("ha")
    raster_rows = token_ids.shape[0]
    full_width = token_ids.shape[1]
    band_rows = raster_rows * across
    band_cols = full_width // across
    raster = embed_ids(token_ids, codebook)
    padded = jnp.pad(raster, ((0, 0), (TILE, TILE), (0, 0)))
    columns = (
        jnp.arange(across, dtype=jnp.int32)[:, None] * band_cols
        + jnp.arange(band_cols + 2 * TILE, dtype=jnp.int32)[None, :]
    )
    windows = jnp.take(padded, columns, axis=1)
    received = lax.all_to_all(windows, "wa", split_axis=1, concat_axis=0, tiled=True)
    band = received.reshape(band_rows, band_cols + 2 * TILE, D)
    widened = with_halo(band, (("ha", 0),), TILE)
    hidden = band[:, TILE : TILE + band_cols]
    total_rows = band_rows * downward
    row_ids = (
        lax.axis_index("ha") * band_rows - TILE + jnp.arange(band_rows + 2 * TILE, dtype=jnp.int32)
    )
    col_ids = (
        lax.axis_index("wa") * band_cols - TILE + jnp.arange(band_cols + 2 * TILE, dtype=jnp.int32)
    )
    inside = ((row_ids >= 0) & (row_ids < total_rows))[:, None] & (
        (col_ids >= 0) & (col_ids < full_width)
    )[None, :]
    query_rows = band_rows // TILE
    query_cols = band_cols // TILE
    key_valid = (
        inside.reshape(query_rows + 2, TILE, query_cols + 2, TILE)
        .transpose(0, 2, 1, 3)
        .reshape((query_rows + 2) * (query_cols + 2), TILE * TILE)
    )
    tile_down = jnp.arange(query_rows, dtype=jnp.int32)[:, None, None]
    tile_across = jnp.arange(query_cols, dtype=jnp.int32)[None, :, None]
    key_index = (
        (tile_down + neighbour_lists // 3) * (query_cols + 2) + tile_across + neighbour_lists % 3
    ).reshape(query_rows * query_cols, NSEL)
    for layer_index in range(BLOCKS):
        hidden = attention_block(
            hidden,
            widened if layer_index == 0 else None,
            key_index,
            key_valid,
            qkv_weight[layer_index],
            out_weight[layer_index],
            logit_scale[layer_index],
        )
    activated = jax.nn.silu(normalize(hidden)).astype(jnp.bfloat16)
    region = with_halo(activated, (("ha", 0), ("wa", 1)), 1)
    running = jnp.zeros((band_rows, band_cols, conv_weight.shape[3]), jnp.float32)
    for shift_row in range(3):
        for shift_col in range(3):
            running = running + jnp.dot(
                region[shift_row : shift_row + band_rows, shift_col : shift_col + band_cols],
                conv_weight[shift_row, shift_col],
                preferred_element_type=jnp.float32,
            )
    return running.astype(jnp.bfloat16)


def solution(mesh):
    in_specs = (
        P(("parts", "ha", "wa"), None),
        P(("parts", "ha"), "wa", None),
        P(),
        P(),
        P(),
        P(),
        P(),
    )
    out_specs = P(("parts", "ha"), "wa", None)
    return jax.shard_map(local, mesh=mesh, in_specs=in_specs, out_specs=out_specs, check_vma=False)
```

profile of v0, /device:TPU:0, one launch (start us, length us, event | category | flops | bytes accessed | tf_op | source)
XLA Modules:
  0.0 118.8 jit_solution(557110675442618728)
XLA Ops:
  0.2 0.7 remainder_compare_fusion.3
  0.9 0.7 broadcast_remainder_fusion
  2.6 0.2 convolution_convert_fusion.2
  3.1 1.1 gather_fusion
  4.2 0.8 fusion.57
  5.0 6.3 %all-to-all-start = ((bf16[2,4,32,512]{3,2,0,1:T(8,128)(2,1)}), bf16[2,4,32,512]{3,2,0,1:T(8,128)(2,1)S(1)}, u32[]{:S(2)}, u32[]{:S(2)}) async-start(bf16[2,4,32,512]{3,2,0,1:T(8,128)(2,1)} %fusion.57), calls=%async_computation | async-start | bytes 524288 | tf_op jit(solution)/shard_map/all_to_all | solution.py:145
  11.7 0.6 gather_fusion.2
  12.3 3.2 %slice_bitcast_fusion = (bf16[512,1536]{1,0:T(8,128)(2,1)}, bf16[512,1536]{1,0:T(8,128)(2,1)S(1)}) fusion(bf16[2,512,1536]{2,1,0:T(8,128)(2,1)} %param.14), kind=kLoop, calls=%fused_computation.17 | loop fusion | bytes 6291456 | tf_op jit(solution)/shard_map/squeeze | solution.py:177
  15.7 4.6 %all-to-all-done = bf16[2,4,32,512]{3,2,0,1:T(8,128)(2,1)S(1)} async-done(((bf16[2,4,32,512]{3,2,0,1:T(8,128)(2,1)}), bf16[2,4,32,512]{3,2,0,1:T(8,128)(2,1)S(1)}, u32[]{:S(2)}, u32[]{:S(2)}) %all-to-all-start) | async-done | bytes 262176 | tf_op jit(solution)/shard_map/all_to_all | solution.py:145
  20.4 1.3 %collective-permute-start.1 = (bf16[8,32,512]{2,1,0:T(8,128)(2,1)S(1)}, bf16[8,32,512]{2,1,0:T(8,128)(2,1)S(1)}, u32[]{:S(2)}, u32[]{:S(2)}) collective-permute-start(bf16[8,32,512]{2,1,0:T(8,128)(2,1)S(1)} %bitcast.198), channel_id=1, source_target_pairs={{4,0},{8,4},{12,8},{5,1},{9,5},{13,9},{6,2},{10,6},{14,10},{7,3},{... | collective-permute-start | bytes 786440 | tf_op jit(solution)/shard_map/ppermute | solution.py:27
  21.7 3.0 %collective-permute-start = (bf16[8,32,512]{2,1,0:T(8,128)(2,1)S(1)}, bf16[8,32,512]{2,1,0:T(8,128)(2,1)S(1)}, u32[]{:S(2)}, u32[]{:S(2)}) collective-permute-start(bf16[8,32,512]{2,1,0:T(8,128)(2,1)S(1)} %bitcast.199), channel_id=1, source_target_pairs={{0,4},{4,8},{8,12},{1,5},{5,9},{9,13},{2,6},{6,10},{10,14},{3,7},{... | collective-permute-start | bytes 786440 | tf_op jit(solution)/shard_map/ppermute | solution.py:26
  24.7 0.3 fusion.137
  25.2 0.2 reduce_sum.93
  25.8 0.9 reshape.429
  26.7 0.2 fusion.4
  26.9 1.0 fusion.22
  28.0 1.1 slice.289
  29.1 0.7 copy-done.5
  29.9 1.4 %slice_multiply_fusion = f32[24,32,512]{2,1,0:T(8,128)} fusion(f32[24,32,1024]{2,1,0:T(8,128)S(1)} %fusion.22), kind=kLoop, calls=%fused_computation.26 | loop fusion | flops 393216 | bytes 3145728 | tf_op jit(solution)/shard_map/mul | solution.py:45
  31.2 2.4 %mul.156 = f32[24,32,8,64]{3,2,1,0:T(8,128)S(1)} reshape(f32[24,32,512]{2,1,0:T(8,128)} %slice_multiply_fusion) | data formatting | bytes 3145728 | tf_op jit(solution)/shard_map/mul | solution.py:45
  33.7 1.7 %reduce_sum.91 = f32[24,32,8]{2,1,0:T(8,128)} reduce(f32[24,32,8,64]{3,2,1,0:T(8,128)S(1)} %mul.156, f32[]{:T(128)} %constant.183.clone.1), dimensions={3}, to_apply=%region_1.2 | reduce | flops 387072 | bytes 1597444 | tf_op jit(solution)/shard_map/reduce_sum | solution.py:45
  35.3 1.1 add_rsqrt_fusion
  36.4 0.9 mul.157
  37.3 1.7 %mul.158 = f32[24,32,512]{2,1,0:T(8,128)} reshape(f32[24,32,8,64]{3,2,1,0:T(8,128)S(1)} %mul.157) | data formatting | bytes 3145728 | tf_op jit(solution)/shard_map/mul | solution.py:45
  39.0 2.2 %multiply_convert_fusion = bf16[24,32,512]{2,1,0:T(8,128)(2,1)S(1)} fusion(f32[24,32,512]{2,1,0:T(8,128)} %mul.158, f32[24,32,1024]{2,1,0:T(8,128)} %copy-done.5), kind=kLoop, calls=%fused_computation.20 | loop fusion | flops 786432 | bytes 3932160 | tf_op jit(solution)/shard_map/convert_element_type | solution.py:50
  41.5 0.6 gather_fusion.1
  42.2 1.4 %broadcast_select_fusion.1 = bf16[2,6,64,1024]{3,2,1,0:T(8,128)(2,1)} fusion(bf16[2,6,64,1024]{3,2,1,0:T(8,128)(2,1)S(1)} %bitcast.196, pred[2,6]{1,0:T(4,128)(4,1)S(1)} %get-tuple-element.6), kind=kLoop, calls=%fused_computation.23 | loop fusion | flops 786432 | bytes 3145740 | tf_op jit(solution)/shard_map/jit(_take)/select_n | solution.py:95
  43.5 4.1 %reshape.428 = bf16[2,384,2,8,64]{4,3,2,1,0:T(8,128)(2,1)S(1)} reshape(bf16[2,6,64,1024]{3,2,1,0:T(8,128)(2,1)} %broadcast_select_fusion.1) | data formatting | bytes 3145728 | tf_op jit(solution)/shard_map/reshape | solution.py:95
  47.7 2.2 %fusion.134 = (bf16[2,384,1,8,64]{4,3,2,1,0:T(8,128)(2,1)}, bf16[2,384,1,8,64]{4,3,2,1,0:T(8,128)(2,1)}) fusion(bf16[2,384,2,8,64]{4,3,2,1,0:T(8,128)(2,1)S(1)} %reshape.428), kind=kLoop, calls=%fused_computation.224 | loop fusion | bytes 3145728 | tf_op jit(solution)/shard_map/slice | solution.py:101
  49.8 2.1 %copy.40 = bf16[2,384,1,8,64]{1,4,3,0,2:T(8,128)(2,1)S(1)} copy(bf16[2,384,1,8,64]{4,3,2,1,0:T(8,128)(2,1)} %get-tuple-element.13) | data formatting | bytes 1572864
  52.0 1.0 copy.39
  53.0 1.6 %fusion.138 = (f32[2,8,64]{2,1,0:T(8,128)S(1)}, f32[2,8,64,384]{3,2,1,0:T(8,128)S(1)}) fusion(bf16[2,384,1,8,64]{1,4,3,0,2:T(8,128)(2,1)S(1)} %copy.40, f32[8]{0:T(128)S(1)} %get-tuple-element.24, pred[2,384]{1,0:T(4,128)(4,1)S(1)} %broadcast_in_dim.48, bf16[1,2,8,8,8,64]{5,4,3,1,2,0:T(8,128)(2,1)} %bitcast.206), kind=kOutput, calls=%fused_computation.228 | convolution fusion | flops 51904896 | bytes 2495264 | tf_op jit(solution)/shard_map/sub | solution.py:107
  54.6 0.5 fusion.8
  55.4 0.2 reshape.431
  55.6 1.4 %multiply_reduce_fusion.1 = (f32[8,16]{1,0:T(8,128)S(1)}, f32[8,16,512]{2,1,0:T(8,128)S(1)}) fusion(bf16[2,512,512]{2,1,0:T(8,128)(2,1)} %param.15, bf16[8,32,512]{2,1,0:T(8,128)(2,1)S(1)} %bitcast.203, bf16[1,2,8,8,512]{4,3,2,1,0:T(8,128)(2,1)S(1)} %reshape.431), kind=kOutput, calls=%fused_computation.109 | convolution fusion | flops 67501952 | bytes 1049088 | tf_op jit(solution)/shard_map/dot_general | solution.py:127
  57.0 0.3 fusion.21
  58.2 0.7 pad_maximum_fusion.5
  58.9 1.3 %collective-permute-start.3 = (bf16[8,16,1024]{2,1,0:T(8,128)(2,1)}, bf16[8,16,1024]{2,1,0:T(8,128)(2,1)S(1)}, u32[]{:S(2)}, u32[]{:S(2)}) collective-permute-start(bf16[8,16,1024]{2,1,0:T(8,128)(2,1)} %pad_maximum_fusion.5), channel_id=1, source_target_pairs={{4,0},{8,4},{12,8},{5,1},{9,5},{13,9},{6,2},{10,6},{14,10},{7,3},{... | collective-permute-start | bytes 786440 | tf_op jit(solution)/shard_map/ppermute | solution.py:27
  60.2 5.0 %collective-permute-start.2 = (bf16[8,16,1024]{2,1,0:T(8,128)(2,1)}, bf16[8,16,1024]{2,1,0:T(8,128)(2,1)S(1)}, u32[]{:S(2)}, u32[]{:S(2)}) collective-permute-start(bf16[8,16,1024]{2,1,0:T(8,128)(2,1)} %pad_maximum_fusion.5), channel_id=1, source_target_pairs={{0,4},{4,8},{8,12},{1,5},{5,9},{9,13},{2,6},{6,10},{10,14},{3,7},{... | collective-permute-start | bytes 786440 | tf_op jit(solution)/shard_map/ppermute | solution.py:26
  65.2 0.3 fusion.143
  65.8 0.7 collective-permute-done.2
  66.6 0.9 fusion.135
  67.5 2.1 %collective-permute-start.4 = (bf16[24,8,1024]{2,1,0:T(8,128)(2,1)}, bf16[24,8,1024]{2,1,0:T(8,128)(2,1)S(1)}, u32[]{:S(2)}, u32[]{:S(2)}) collective-permute-start(bf16[24,8,1024]{2,1,0:T(8,128)(2,1)} %get-tuple-element.15), channel_id=1, source_target_pairs={{0,1},{1,2},{2,3},{4,5},{5,6},{6,7},{8,9},{9,10},{10,11},{12,13},{... | collective-permute-start | bytes 1179656 | tf_op jit(solution)/shard_map/ppermute | solution.py:26
  69.6 1.5 %collective-permute-start.5 = (bf16[24,8,1024]{2,1,0:T(8,128)(2,1)}, bf16[24,8,1024]{2,1,0:T(8,128)(2,1)S(1)}, u32[]{:S(2)}, u32[]{:S(2)}) collective-permute-start(bf16[24,8,1024]{2,1,0:T(8,128)(2,1)} %get-tuple-element.16), channel_id=1, source_target_pairs={{1,0},{2,1},{3,2},{5,4},{6,5},{7,6},{9,8},{10,9},{11,10},{13,12},{... | collective-permute-start | bytes 1179656 | tf_op jit(solution)/shard_map/ppermute | solution.py:27
  71.5 0.9 reshape.436
  72.4 3.2 %collective-permute-done.4 = bf16[24,8,1024]{2,1,0:T(8,128)(2,1)S(1)} collective-permute-done((bf16[24,8,1024]{2,1,0:T(8,128)(2,1)}, bf16[24,8,1024]{2,1,0:T(8,128)(2,1)S(1)}, u32[]{:S(2)}, u32[]{:S(2)}) %collective-permute-start.4) | collective-permute-done | bytes 393248 | tf_op jit(solution)/shard_map/ppermute | solution.py:26
  75.6 4.6 %collective-permute-done.5 = bf16[24,8,1024]{2,1,0:T(8,128)(2,1)S(1)} collective-permute-done((bf16[24,8,1024]{2,1,0:T(8,128)(2,1)}, bf16[24,8,1024]{2,1,0:T(8,128)(2,1)S(1)}, u32[]{:S(2)}, u32[]{:S(2)}) %collective-permute-start.5) | collective-permute-done | bytes 393248 | tf_op jit(solution)/shard_map/ppermute | solution.py:27
  80.5 0.6 gather_fusion.3
  81.2 1.4 %broadcast_select_fusion = bf16[2,6,64,1024]{3,2,1,0:T(8,128)(2,1)} fusion(bf16[2,6,64,1024]{3,2,1,0:T(8,128)(2,1)S(1)} %bitcast.195, pred[2,6]{1,0:T(4,128)(4,1)S(1)} %get-tuple-element.6), kind=kLoop, calls=%fused_computation.22 | loop fusion | flops 786432 | bytes 3145740 | tf_op jit(solution)/shard_map/jit(_take)/select_n | solution.py:95
  82.6 4.1 %reshape.435 = bf16[2,384,2,8,64]{4,3,2,1,0:T(8,128)(2,1)S(1)} reshape(bf16[2,6,64,1024]{3,2,1,0:T(8,128)(2,1)} %broadcast_select_fusion) | data formatting | bytes 3145728 | tf_op jit(solution)/shard_map/reshape | solution.py:95
  86.7 2.2 %fusion.133 = (bf16[2,384,1,8,64]{4,3,2,1,0:T(8,128)(2,1)}, bf16[2,384,1,8,64]{4,3,2,1,0:T(8,128)(2,1)}) fusion(bf16[2,384,2,8,64]{4,3,2,1,0:T(8,128)(2,1)S(1)} %reshape.435), kind=kLoop, calls=%fused_computation.223 | loop fusion | bytes 3145728 | tf_op jit(solution)/shard_map/slice | solution.py:101
  88.9 2.1 %copy.42 = bf16[2,384,1,8,64]{1,4,3,0,2:T(8,128)(2,1)S(1)} copy(bf16[2,384,1,8,64]{4,3,2,1,0:T(8,128)(2,1)} %get-tuple-element.9) | data formatting | bytes 1572864
  91.0 1.0 copy.41
  92.1 1.8 %fusion.144 = (f32[2,8,64]{2,1,0:T(8,128)S(1)}, f32[2,8,64,384]{3,2,1,0:T(8,128)}) fusion(bf16[2,384,1,8,64]{1,4,3,0,2:T(8,128)(2,1)S(1)} %copy.42, f32[8]{0:T(128)S(1)} %get-tuple-element.23, pred[2,384]{1,0:T(4,128)(4,1)S(1)} %broadcast_in_dim.48, bf16[1,2,8,8,8,64]{5,4,3,1,2,0:T(8,128)(2,1)S(1)} %bitcast.207), kind=kOutput, calls=%fused_computation.230 | convolution fusion | flops 51904896 | bytes 2495264 | tf_op jit(solution)/shard_map/sub | solution.py:107
  93.8 2.0 %fusion.9 = bf16[2,64,8,64]{1,3,2,0:T(8,128)(2,1)S(1)} fusion(bf16[2,384,1,8,64]{1,4,3,0,2:T(8,128)(2,1)S(1)} %copy.41, f32[2,8,64,384]{3,2,1,0:T(8,128)} %get-tuple-element.51, f32[2,8,64]{2,1,0:T(8,128)S(1)} %get-tuple-element.50), kind=kOutput, calls=%fused_computation.32 | convolution fusion | flops 51183616 | bytes 2494464 | tf_op jit(solution)/shard_map/thqk,tkhd->tqhd/dot_general | solution.py:109
  96.0 0.2 reshape.438
  96.2 1.6 %multiply_reduce_fusion = (f32[8,16]{1,0:T(8,128)S(1)}, f32[8,16,512]{2,1,0:T(8,128)S(1)}) fusion(f32[8,16,512]{2,1,0:T(8,128)S(1)} %copy-done.8, bf16[2,512,512]{2,1,0:T(8,128)(2,1)} %param.15, bf16[1,2,8,8,512]{4,3,2,1,0:T(8,128)(2,1)S(1)} %reshape.438), kind=kOutput, calls=%fused_computation.105 | convolution fusion | flops 67436416 | bytes 1180160 | tf_op jit(solution)/shard_map/dot_general | solution.py:127
  98.0 5.2 %collective-permute-start.6 = (bf16[1,16,512]{2,1,0:T(8,128)(2,1)S(1)}, bf16[1,16,512]{2,1,0:T(8,128)(2,1)S(1)}, u32[]{:S(2)}, u32[]{:S(2)}) collective-permute-start(bf16[1,16,512]{2,1,0:T(8,128)(2,1)S(1)} %get-tuple-element.21), channel_id=1, source_target_pairs={{0,4},{4,8},{8,12},{1,5},{5,9},{9,13},{2,6},{6,10},{10,14},{3,7},{... | collective-permute-start | bytes 49160 | tf_op jit(solution)/shard_map/ppermute | solution.py:26
  103.2 1.3 %collective-permute-start.7 = (bf16[1,16,512]{2,1,0:T(8,128)(2,1)S(1)}, bf16[1,16,512]{2,1,0:T(8,128)(2,1)S(1)}, u32[]{:S(2)}, u32[]{:S(2)}) collective-permute-start(bf16[1,16,512]{2,1,0:T(8,128)(2,1)S(1)} %get-tuple-element.22), channel_id=1, source_target_pairs={{4,0},{8,4},{12,8},{5,1},{9,5},{13,9},{6,2},{10,6},{14,10},{7,3},{... | collective-permute-start | bytes 49160 | tf_op jit(solution)/shard_map/ppermute | solution.py:27
  104.7 4.2 %collective-permute-done.7 = bf16[1,16,512]{2,1,0:T(8,128)(2,1)S(1)} collective-permute-done((bf16[1,16,512]{2,1,0:T(8,128)(2,1)S(1)}, bf16[1,16,512]{2,1,0:T(8,128)(2,1)S(1)}, u32[]{:S(2)}, u32[]{:S(2)}) %collective-permute-start.7) | collective-permute-done | bytes 16416 | tf_op jit(solution)/shard_map/ppermute | solution.py:27
  108.9 2.3 %collective-permute-start.8 = (bf16[10,1,512]{2,1,0:T(2,128)(2,1)S(1)}, bf16[10,1,512]{2,1,0:T(2,128)(2,1)S(1)}, u32[]{:S(2)}, u32[]{:S(2)}) collective-permute-start(bf16[10,1,512]{2,1,0:T(2,128)(2,1)S(1)} %get-tuple-element.19), channel_id=1, source_target_pairs={{0,1},{1,2},{2,3},{4,5},{5,6},{6,7},{8,9},{9,10},{10,11},{12,13},{... | collective-permute-start | bytes 30728 | tf_op jit(solution)/shard_map/ppermute | solution.py:26
  111.2 1.3 %collective-permute-start.9 = (bf16[10,1,512]{2,1,0:T(2,128)(2,1)S(1)}, bf16[10,1,512]{2,1,0:T(2,128)(2,1)S(1)}, u32[]{:S(2)}, u32[]{:S(2)}) collective-permute-start(bf16[10,1,512]{2,1,0:T(2,128)(2,1)S(1)} %get-tuple-element.20), channel_id=1, source_target_pairs={{1,0},{2,1},{3,2},{5,4},{6,5},{7,6},{9,8},{10,9},{11,10},{13,12},{... | collective-permute-start | bytes 30728 | tf_op jit(solution)/shard_map/ppermute | solution.py:27
  112.9 4.0 %collective-permute-done.9 = bf16[10,1,512]{2,1,0:T(2,128)(2,1)S(1)} collective-permute-done((bf16[10,1,512]{2,1,0:T(2,128)(2,1)S(1)}, bf16[10,1,512]{2,1,0:T(2,128)(2,1)S(1)}, u32[]{:S(2)}, u32[]{:S(2)}) %collective-permute-start.9) | collective-permute-done | bytes 10272 | tf_op jit(solution)/shard_map/ppermute | solution.py:27
  117.9 0.8 fusion.20
  (103 shorter events, 7.0 us)
Async XLA Ops:
  0.0 2.6 %copy-start = (bf16[39,512]{1,0:T(8,128)(2,1)S(1)}, bf16[39,512]{1,0:T(8,128)(2,1)}, u32[]{:S(2)}) copy-start(bf16[39,512]{1,0:T(8,128)(2,1)} %param.13) | copy-start | bytes 119812
  0.0 11.4 %copy-start.11 = (s32[1,2,6]{2,1,0:T(2,128)S(1)}, s32[1,2,6]{2,1,0:T(2,128)}, u32[]{:S(2)}) copy-start(s32[1,2,6]{2,1,0:T(2,128)} %param.12) | copy-start | bytes 148
  5.0 15.3 %all-to-all-start = ((bf16[2,4,32,512]{3,2,0,1:T(8,128)(2,1)}), bf16[2,4,32,512]{3,2,0,1:T(8,128)(2,1)S(1)}, u32[]{:S(2)}, u32[]{:S(2)}) async-start(bf16[2,4,32,512]{3,2,0,1:T(8,128)(2,1)} %fusion.57), calls=%async_computation | async-start | bytes 524288 | tf_op jit(solution)/shard_map/all_to_all | solution.py:145
  12.3 3.4 %copy-start.12 = (f32[2,8]{1,0:T(2,128)S(1)}, f32[2,8]{1,0:T(2,128)}, u32[]{:S(2)}) copy-start(f32[2,8]{1,0:T(2,128)} %param.16) | copy-start | bytes 196
  20.4 6.3 %collective-permute-start.1 = (bf16[8,32,512]{2,1,0:T(8,128)(2,1)S(1)}, bf16[8,32,512]{2,1,0:T(8,128)(2,1)S(1)}, u32[]{:S(2)}, u32[]{:S(2)}) collective-permute-start(bf16[8,32,512]{2,1,0:T(8,128)(2,1)S(1)} %bitcast.198), channel_id=1, source_target_pairs={{4,0},{8,4},{12,8},{5,1},{9,5},{13,9},{6,2},{10,6},{14,10},{7,3},{... | collective-permute-start | bytes 786440 | tf_op jit(solution)/shard_map/ppermute | solution.py:27
  21.7 5.0 %collective-permute-start = (bf16[8,32,512]{2,1,0:T(8,128)(2,1)S(1)}, bf16[8,32,512]{2,1,0:T(8,128)(2,1)S(1)}, u32[]{:S(2)}, u32[]{:S(2)}) collective-permute-start(bf16[8,32,512]{2,1,0:T(8,128)(2,1)S(1)} %bitcast.199), channel_id=1, source_target_pairs={{0,4},{4,8},{8,12},{1,5},{5,9},{9,13},{2,6},{6,10},{10,14},{3,7},{... | collective-permute-start | bytes 786440 | tf_op jit(solution)/shard_map/ppermute | solution.py:26
  28.0 1.9 %copy-start.5 = (f32[24,32,1024]{2,1,0:T(8,128)}, f32[24,32,1024]{2,1,0:T(8,128)S(1)}, u32[]{:S(2)}) copy-start(f32[24,32,1024]{2,1,0:T(8,128)S(1)} %fusion.22) | copy-start | bytes 9437188
  39.0 2.2 %copy-start.6 = (bf16[24,32,512]{2,1,0:T(8,128)(2,1)S(1)}, bf16[24,32,512]{2,1,0:T(8,128)(2,1)}, u32[]{:S(2)}) copy-start(bf16[24,32,512]{2,1,0:T(8,128)(2,1)} %slice.289) | copy-start | bytes 2359300
  49.8 2.1 %copy-start.3 = (bf16[2,384,1,8,64]{4,3,2,1,0:T(8,128)(2,1)S(1)}, bf16[2,384,1,8,64]{4,3,2,1,0:T(8,128)(2,1)}, u32[]{:S(2)}) copy-start(bf16[2,384,1,8,64]{4,3,2,1,0:T(8,128)(2,1)} %get-tuple-element.14) | copy-start | bytes 2359300
  55.1 1.9 %copy-start.2 = (bf16[512,1536]{1,0:T(8,128)(2,1)S(1)}, bf16[512,1536]{1,0:T(8,128)(2,1)}, u32[]{:S(2)}) copy-start(bf16[512,1536]{1,0:T(8,128)(2,1)} %get-tuple-element.11) | copy-start | bytes 4718596
  57.0 8.2 %copy-start.7 = (f32[8,16,512]{2,1,0:T(8,128)}, f32[8,16,512]{2,1,0:T(8,128)S(1)}, u32[]{:S(2)}) copy-start(f32[8,16,512]{2,1,0:T(8,128)S(1)} %get-tuple-element.47) | copy-start | bytes 786436
  58.9 6.9 %collective-permute-start.3 = (bf16[8,16,1024]{2,1,0:T(8,128)(2,1)}, bf16[8,16,1024]{2,1,0:T(8,128)(2,1)S(1)}, u32[]{:S(2)}, u32[]{:S(2)}) collective-permute-start(bf16[8,16,1024]{2,1,0:T(8,128)(2,1)} %pad_maximum_fusion.5), channel_id=1, source_target_pairs={{4,0},{8,4},{12,8},{5,1},{9,5},{13,9},{6,2},{10,6},{14,10},{7,3},{... | collective-permute-start | bytes 786440 | tf_op jit(solution)/shard_map/ppermute | solution.py:27
  60.2 6.3 %collective-permute-start.2 = (bf16[8,16,1024]{2,1,0:T(8,128)(2,1)}, bf16[8,16,1024]{2,1,0:T(8,128)(2,1)S(1)}, u32[]{:S(2)}, u32[]{:S(2)}) collective-permute-start(bf16[8,16,1024]{2,1,0:T(8,128)(2,1)} %pad_maximum_fusion.5), channel_id=1, source_target_pairs={{0,4},{4,8},{8,12},{1,5},{5,9},{9,13},{2,6},{6,10},{10,14},{3,7},{... | collective-permute-start | bytes 786440 | tf_op jit(solution)/shard_map/ppermute | solution.py:26
  67.5 8.1 %collective-permute-start.4 = (bf16[24,8,1024]{2,1,0:T(8,128)(2,1)}, bf16[24,8,1024]{2,1,0:T(8,128)(2,1)S(1)}, u32[]{:S(2)}, u32[]{:S(2)}) collective-permute-start(bf16[24,8,1024]{2,1,0:T(8,128)(2,1)} %get-tuple-element.15), channel_id=1, source_target_pairs={{0,1},{1,2},{2,3},{4,5},{5,6},{6,7},{8,9},{9,10},{10,11},{12,13},{... | collective-permute-start | bytes 1179656 | tf_op jit(solution)/shard_map/ppermute | solution.py:26
  69.6 10.6 %collective-permute-start.5 = (bf16[24,8,1024]{2,1,0:T(8,128)(2,1)}, bf16[24,8,1024]{2,1,0:T(8,128)(2,1)S(1)}, u32[]{:S(2)}, u32[]{:S(2)}) collective-permute-start(bf16[24,8,1024]{2,1,0:T(8,128)(2,1)} %get-tuple-element.16), channel_id=1, source_target_pairs={{1,0},{2,1},{3,2},{5,4},{6,5},{7,6},{9,8},{10,9},{11,10},{13,12},{... | collective-permute-start | bytes 1179656 | tf_op jit(solution)/shard_map/ppermute | solution.py:27
  88.9 2.2 %copy-start.4 = (bf16[2,384,1,8,64]{4,3,2,1,0:T(8,128)(2,1)S(1)}, bf16[2,384,1,8,64]{4,3,2,1,0:T(8,128)(2,1)}, u32[]{:S(2)}) copy-start(bf16[2,384,1,8,64]{4,3,2,1,0:T(8,128)(2,1)} %get-tuple-element.10) | copy-start | bytes 2359300
  91.0 1.0 copy-start.10
  93.8 2.4 %copy-start.8 = (f32[8,16,512]{2,1,0:T(8,128)S(1)}, f32[8,16,512]{2,1,0:T(8,128)}, u32[]{:S(2)}) copy-start(f32[8,16,512]{2,1,0:T(8,128)} %copy-done.7) | copy-start | bytes 786436
  95.8 8.7 %copy-start.9 = (bf16[3,3,512,256]{3,2,1,0:T(8,128)(2,1)S(1)}, bf16[3,3,512,256]{3,2,1,0:T(8,128)(2,1)}, u32[]{:S(2)}) copy-start(bf16[3,3,512,256]{3,2,1,0:T(8,128)(2,1)} %param.17) | copy-start | bytes 7077892
  98.0 6.7 %collective-permute-start.6 = (bf16[1,16,512]{2,1,0:T(8,128)(2,1)S(1)}, bf16[1,16,512]{2,1,0:T(8,128)(2,1)S(1)}, u32[]{:S(2)}, u32[]{:S(2)}) collective-permute-start(bf16[1,16,512]{2,1,0:T(8,128)(2,1)S(1)} %get-tuple-element.21), channel_id=1, source_target_pairs={{0,4},{4,8},{8,12},{1,5},{5,9},{9,13},{2,6},{6,10},{10,14},{3,7},{... | collective-permute-start | bytes 49160 | tf_op jit(solution)/shard_map/ppermute | solution.py:26
  103.2 5.7 %collective-permute-start.7 = (bf16[1,16,512]{2,1,0:T(8,128)(2,1)S(1)}, bf16[1,16,512]{2,1,0:T(8,128)(2,1)S(1)}, u32[]{:S(2)}, u32[]{:S(2)}) collective-permute-start(bf16[1,16,512]{2,1,0:T(8,128)(2,1)S(1)} %get-tuple-element.22), channel_id=1, source_target_pairs={{4,0},{8,4},{12,8},{5,1},{9,5},{13,9},{6,2},{10,6},{14,10},{7,3},{... | collective-permute-start | bytes 49160 | tf_op jit(solution)/shard_map/ppermute | solution.py:27
  108.9 4.0 %collective-permute-start.8 = (bf16[10,1,512]{2,1,0:T(2,128)(2,1)S(1)}, bf16[10,1,512]{2,1,0:T(2,128)(2,1)S(1)}, u32[]{:S(2)}, u32[]{:S(2)}) collective-permute-start(bf16[10,1,512]{2,1,0:T(2,128)(2,1)S(1)} %get-tuple-element.19), channel_id=1, source_target_pairs={{0,1},{1,2},{2,3},{4,5},{5,6},{6,7},{8,9},{9,10},{10,11},{12,13},{... | collective-permute-start | bytes 30728 | tf_op jit(solution)/shard_map/ppermute | solution.py:26
  111.2 5.7 %collective-permute-start.9 = (bf16[10,1,512]{2,1,0:T(2,128)(2,1)S(1)}, bf16[10,1,512]{2,1,0:T(2,128)(2,1)S(1)}, u32[]{:S(2)}, u32[]{:S(2)}) collective-permute-start(bf16[10,1,512]{2,1,0:T(2,128)(2,1)S(1)} %get-tuple-element.20), channel_id=1, source_target_pairs={{1,0},{2,1},{3,2},{5,4},{6,5},{7,6},{9,8},{10,9},{11,10},{13,12},{... | collective-permute-start | bytes 30728 | tf_op jit(solution)/shard_map/ppermute | solution.py:27
  117.3 1.4 %copy-start.1 = (bf16[39,512]{1,0:T(8,128)(2,1)S(1)}, bf16[39,512]{1,0:T(8,128)(2,1)}, u32[]{:S(2)}) copy-start(bf16[39,512]{1,0:T(8,128)(2,1)} %param.13) | copy-start | bytes 119812
where the time goes:
time: 120 us; the launch traced here: 119 us
  local copies, waits for them, and re-layouts  38.9 us (32%)
  starting transfers between devices  30.5 us (25%)
  waiting for transfers between devices  21.2 us (18%)
  other arithmetic  14.1 us (12%)
  matrix products  13.3 us (11%)
    ppermute x5, starting transfers between devices, with_halo(): before = lax.ppermute(last, axis, up)  17.5 us
    ppermute x5, waiting for transfers between devices, with_halo(): after = lax.ppermute(initial, axis, down)  12.7 us
    reshape x2, local copies, waits for them, and re-layouts, attend(): jnp.take(region_tiles, key_index, axis=0)  8.24 us
    unnamed x30, local copies, waits for them, and re-layouts  7.06 us
    ppermute x5, starting transfers between devices, with_halo(): after = lax.ppermute(initial, axis, down)  6.63 us
    all_to_all x1, starting transfers between devices, local(): lax.all_to_all(windows, 'wa', split_axis=1, concat_axis=0, tiled=True)  6.35 us
    all_to_all x1, waiting for transfers between devices, local(): lax.all_to_all(windows, 'wa', split_axis=1, concat_axis=0, tiled=True)  4.56 us
    slice x2, local copies, waits for them, and re-layouts, attend(): gathered[:, :, 0]  4.37 us
  transfers between devices with their start and end apart: 11, of which 6 were waited for; matrix products, arithmetic and copies ran while one was open for 7% of the time, Pallas kernels for 0%

commit v1 on v0

v1 whole, which is shorter than its diff:
```python
import functools
import math

import jax
import jax.numpy as jnp
from jax import lax
from jax.experimental import pallas as pl
from jax.experimental.pallas import tpu as pltpu
from jax.sharding import PartitionSpec as P

D = 512
HEADS = 8
HEAD = D // HEADS
TILE = 8
AREA = TILE * TILE
NSEL = 6
BLOCKS = 2
HALF = 256
GROUP = HALF // HEAD
digit_levels = (8, 8, 8, 5, 5, 5)
digit_shift = (6, 3, 0, 9, 12, 15)
norm_eps = 1e-06
LOG2E = math.log2(math.e)
NEG = -1e30

f32 = jnp.float32
bf16 = jnp.bfloat16
i32 = jnp.int32


def mm(a, b):
    return lax.dot_general(a, b, (((1,), (0,)), ((), ())), preferred_element_type=f32)


def mm_t(a, b):
    return lax.dot_general(a, b, (((1,), (1,)), ((), ())), preferred_element_type=f32)


def tiles_at_once(count):
    return max(n for n in range(1, 5) if count % n == 0)


def pack_digits(ids):
    x = ids.astype(f32)
    q5 = jnp.floor((x + 0.5) * 0.2)
    q4 = jnp.floor((q5 + 0.5) * 0.2)
    q3 = jnp.floor((q4 + 0.5) * 0.2)
    return q3 + 512.0 * (q4 - 5.0 * q3) + 4096.0 * (q5 - 5.0 * q4) + 32768.0 * (x - 5.0 * q5)


def slot_tables():
    lane = lax.broadcasted_iota(i32, (1, 128), 1)
    slot = lane & 63
    shift = jnp.zeros_like(lane)
    start = jnp.zeros_like(lane)
    offset = 0
    for size, bits in zip(digit_levels, digit_shift):
        here = slot >= offset
        shift = jnp.where(here, bits, shift)
        start = jnp.where(here, offset, start)
        offset += size
    return shift, jnp.where(slot < offset, slot - start, -1)


def head_scale(x, ones_bd, floor):
    parts = []
    for half in range(D // HALF):
        piece = x[:, HALF * half : HALF * half + HALF]
        total = mm((piece * piece).astype(bf16), ones_bd)
        parts.append((piece * lax.rsqrt(total * (1.0 / HEAD) + floor)).astype(bf16))
    return jnp.concatenate(parts, axis=1)


def square_mean(x):
    return jnp.sum(x * x, axis=-1, keepdims=True) * (1.0 / D)


def attend_tile(q, starts, bias, factors, keys, values, lane_head):
    outs = []
    for g in range(D // HALF):
        cols = slice(HALF * g, HALF * g + HALF)
        qg = q[:, cols]
        q_bd = jnp.concatenate(
            [jnp.where(lane_head == h, qg, jnp.zeros_like(qg)) for h in range(GROUP)], axis=0
        )
        k = jnp.concatenate([keys[pl.ds(s, AREA), cols] for s in starts], axis=0)
        v = jnp.concatenate([values[pl.ds(s, AREA), cols] for s in starts], axis=0)
        s = mm_t(q_bd, k) + bias
        s = s - jnp.max(s, axis=-1, keepdims=True)
        p = jnp.concatenate(
            [
                jnp.exp2(s[AREA * h : AREA * h + AREA] * factors[GROUP * g + h])
                for h in range(GROUP)
            ],
            axis=0,
        )
        den = jnp.sum(p, axis=-1, keepdims=True)
        o = mm(p.astype(bf16), v) * (1.0 / den)
        r = o[:AREA]
        for h in range(1, GROUP):
            r = jnp.where(lane_head == h, o[AREA * h : AREA * h + AREA], r)
        outs.append(r)
    return jnp.concatenate(outs, axis=1).astype(bf16)


def body(
    geo,
    lists_ref, place_ref, scale_ref, ids_ref, table_ref, book_ref, wq_hbm, wo_hbm, wc_hbm,
    out_ref,
    onehot, hid0, q0, k0, v0, att, hid1, q1, k1, v1, region, wq, wo, wc, sems,
):
    tr, tc, r0n, c0n, r1n, c1n, qr, qc, rr, width = geo
    copies = [
        pltpu.make_async_copy(wo_hbm, wo, sems.at[0]),
        pltpu.make_async_copy(wq_hbm.at[1], wq, sems.at[1]),
        pltpu.make_async_copy(wc_hbm, wc, sems.at[2]),
    ]
    for copy in copies:
        copy.start()
    own_r, own_c = place_ref[0], place_ref[1]
    r0, c0, r1, c1 = (place_ref[n] for n in range(2, 6))
    lane_head = lax.broadcasted_iota(i32, (1, HALF), 1) // HEAD
    ones_bd = (
        lax.broadcasted_iota(i32, (HALF, HALF), 0) // HEAD
        == lax.broadcasted_iota(i32, (HALF, HALF), 1) // HEAD
    ).astype(f32).astype(bf16)

    shift, digit = slot_tables()
    lanes = ids_ref.shape[1]
    place = lax.broadcasted_iota(i32, (AREA, lanes), 0)
    rel = (
        lax.broadcasted_iota(i32, (AREA, lanes), 1)
        - (place // TILE) % rr * width
        - place % TILE
    )
    packed = pack_digits(ids_ref[...])
    per_tile = TILE // rr
    for i in range(r1n):
        spread = jnp.concatenate(
            [
                jnp.broadcast_to(packed[n : n + 1], (TILE * rr, lanes))
                for n in range(i * per_tile, (i + 1) * per_tile)
            ],
            axis=0,
        )
        for j in range(c1n):
            mine = jnp.where(rel == TILE * (c1 + j), spread, 0.0)
            code = jnp.sum(mine, axis=-1, keepdims=True).astype(i32)
            hit = (lax.shift_right_logical(jnp.broadcast_to(code, (AREA, 128)), shift) & 7) == digit
            t = i * c1n + j
            onehot[AREA * t : AREA * t + AREA, :] = hit.astype(f32).astype(bf16)

    step1 = tiles_at_once(r1n * c1n)
    chunk1 = step1 * AREA

    def project0(n, _):
        rows = pl.ds(pl.multiple_of(n * chunk1, chunk1), chunk1)
        oh = onehot[rows, :]
        hid = mm(oh, book_ref[...]).astype(bf16)
        hid0[rows, :] = hid
        ms = square_mean(hid.astype(f32)) + norm_eps
        floor = norm_eps * ms
        q0[rows, :] = head_scale(mm(oh, table_ref[:, :D]), ones_bd, floor)
        k0[rows, :] = head_scale(mm(oh, table_ref[:, D : 2 * D]), ones_bd, floor)
        v0[rows, :] = (mm(oh, table_ref[:, 2 * D :]) * lax.rsqrt(ms)).astype(bf16)
        return 0

    lax.fori_loop(0, r1n * c1n // step1, project0, 0)

    bias_tile = lax.broadcasted_iota(i32, (1, NSEL * AREA), 1) // AREA

    def neighbours(gi, gj, row0, col0, cols):
        gi = jnp.clip(gi, 0, tr - 1)
        gj = jnp.clip(gj, 0, tc - 1)
        owner = gi // qr * (tc // qc) + gj // qc
        at = (gi % qr * qc + gj % qc) * NSEL
        starts = []
        bias = jnp.zeros((1, NSEL * AREA), f32)
        for n in range(NSEL):
            number = lists_ref[owner, at + n]
            ni = gi - 1 + number // 3
            nj = gj - 1 + number % 3
            inside = (ni >= 0) & (ni < tr) & (nj >= 0) & (nj < tc)
            ni = jnp.where(inside, ni, gi)
            nj = jnp.where(inside, nj, gj)
            starts.append(pl.multiple_of(((ni - row0) * cols + nj - col0) * AREA, AREA))
            bias = jnp.where(bias_tile == n, jnp.where(inside, 0.0, NEG), bias)
        return starts, bias

    def factors_of(layer):
        return [scale_ref[layer, h] * (LOG2E / math.sqrt(HEAD)) for h in range(HEADS)]

    fac0 = factors_of(0)

    def in_window0(t):
        return ((r0 - r1 + t // c0n) * c1n + (c0 - c1 + t % c0n)) * AREA

    step0 = tiles_at_once(r0n * c0n)
    chunk0 = step0 * AREA

    def attend0(m, _):
        for u in range(step0):
            t = m * step0 + u
            gi, gj = r0 + t // c0n, c0 + t % c0n
            starts, bias = neighbours(gi, gj, r1, c1, c1n)
            q = q0[pl.ds(pl.multiple_of(in_window0(t), AREA), AREA), :]
            att[pl.ds(pl.multiple_of(t * AREA, AREA), AREA), :] = attend_tile(
                q, starts, bias, fac0, k0, v0, lane_head
            )
        return 0

    lax.fori_loop(0, r0n * c0n // step0, attend0, 0)

    copies[0].wait()
    copies[1].wait()

    def project1(n, _):
        rows = pl.ds(pl.multiple_of(n * chunk0, chunk0), chunk0)
        old = jnp.concatenate(
            [
                hid0[pl.ds(pl.multiple_of(in_window0(n * step0 + u), AREA), AREA), :]
                for u in range(step0)
            ],
            axis=0,
        )
        hid = (old.astype(f32) + mm(att[rows, :], wo[0])).astype(bf16)
        hid1[rows, :] = hid
        ms = square_mean(hid.astype(f32)) + norm_eps
        floor = norm_eps * ms
        q1[rows, :] = head_scale(mm(hid, wq[:, :D]), ones_bd, floor)
        k1[rows, :] = head_scale(mm(hid, wq[:, D : 2 * D]), ones_bd, floor)
        v1[rows, :] = (mm(hid, wq[:, 2 * D :]) * lax.rsqrt(ms)).astype(bf16)
        return 0

    lax.fori_loop(0, r0n * c0n // step0, project1, 0)

    fac1 = factors_of(1)
    ring_r, ring_c = qr + 2, qc + 2

    def ring_row(i, _):
        gi = own_r - 1 + i
        for j in range(ring_c):
            gj = own_c - 1 + j
            starts, bias = neighbours(gi, gj, r0, c0, c0n)
            ci = jnp.clip(gi, 0, tr - 1)
            cj = jnp.clip(gj, 0, tc - 1)
            here = pl.ds(pl.multiple_of(((ci - r0) * c0n + cj - c0) * AREA, AREA), AREA)
            tile = attend_tile(q1[here, :], starts, bias, fac1, k1, v1, lane_head)
            att[pl.ds(pl.multiple_of((i * ring_c + j) * AREA, AREA), AREA), :] = tile
        return 0

    lax.fori_loop(0, ring_r, ring_row, 0)

    def finish_row(i, _):
        gi = own_r - 1 + i
        for j in range(ring_c):
            gj = own_c - 1 + j
            inside = (gi >= 0) & (gi < tr) & (gj >= 0) & (gj < tc)
            ci = jnp.clip(gi, 0, tr - 1)
            cj = jnp.clip(gj, 0, tc - 1)
            here = pl.ds(pl.multiple_of(((ci - r0) * c0n + cj - c0) * AREA, AREA), AREA)
            tile = att[pl.ds(pl.multiple_of((i * ring_c + j) * AREA, AREA), AREA), :]
            hid = (hid1[here, :].astype(f32) + mm(tile, wo[1])).astype(bf16).astype(f32)
            v = hid * lax.rsqrt(square_mean(hid) + norm_eps)
            act = jnp.where(inside, v / (1.0 + jnp.exp(-v)), 0.0)
            for r in range(TILE):
                region[pl.ds(i * TILE + r, 1), TILE * j : TILE * j + TILE, :] = act[
                    TILE * r : TILE * r + TILE
                ][None]
        return 0

    lax.fori_loop(0, ring_r, finish_row, 0)

    copies[2].wait()
    rows, cols = qr * TILE, qc * TILE
    total = jnp.zeros((rows * cols, wc.shape[-1]), f32)
    for dc in range(3):
        left = TILE - 1 + dc
        shifted = region[TILE - 1 : TILE + rows + 1, left : left + cols, :].astype(bf16)
        for dr in range(3):
            piece = shifted[dr : dr + rows].reshape(rows * cols, D)
            total = total + mm(piece, wc[dr, dc])
    out_ref[...] = total.astype(bf16).reshape(rows, cols, wc.shape[-1])


def table_body(book_ref, w_ref, table_ref, padded_ref):
    book = book_ref[...]
    full = mm(book, w_ref[0])
    high = full.astype(bf16)
    low = (full - high.astype(f32)).astype(bf16)
    table_ref[...] = jnp.concatenate([high, low], axis=0)
    padded_ref[...] = jnp.concatenate([book, jnp.zeros_like(book)], axis=0)


def local(token_ids, neighbour_lists, codebook, qkv_weight, out_weight, logit_scale, conv_weight):
    across = lax.axis_size("wa")
    down = lax.axis_size("ha")
    rr, width = token_ids.shape
    qr, qc = neighbour_lists.shape[:2]
    tr, tc = qr * down, qc * across
    assert TILE % rr == 0
    ids = token_ids.reshape(1, rr * width)
    lists = neighbour_lists.reshape(1, -1)
    id_lanes = -(-ids.shape[1] // 128) * 128
    list_lanes = -(-lists.shape[1] // 128) * 128
    row = jnp.concatenate(
        [
            jnp.pad(ids, ((0, 0), (0, id_lanes - ids.shape[1]))),
            jnp.pad(lists, ((0, 0), (0, list_lanes - lists.shape[1]))),
        ],
        axis=1,
    )
    group = down * across
    everyone = lax.all_to_all(
        jnp.broadcast_to(row, (group, row.shape[1])), ("ha", "wa"), 0, 0, tiled=True
    )

    own_r = lax.axis_index("ha") * qr
    own_c = lax.axis_index("wa") * qc
    r0n, c0n = min(qr + 4, tr), min(qc + 4, tc)
    r1n, c1n = min(r0n + 2, tr), min(c0n + 2, tc)
    r0 = jnp.clip(own_r - 2, 0, tr - r0n)
    c0 = jnp.clip(own_c - 2, 0, tc - c0n)
    r1 = jnp.clip(r0 - 1, 0, tr - r1n)
    c1 = jnp.clip(c0 - 1, 0, tc - c1n)
    place = jnp.stack([own_r, own_c, r0, c0, r1, c1]).astype(i32)
    id_rows = r1n * TILE // rr
    window = everyone
    if id_rows != group:
        window = lax.dynamic_slice_in_dim(everyone, r1 * TILE // rr, id_rows, axis=0)

    book = jnp.pad(codebook, ((0, 64 - codebook.shape[0]), (0, 0)))
    vmem = pl.BlockSpec(memory_space=pltpu.VMEM)
    smem = pl.BlockSpec(memory_space=pltpu.SMEM)
    hbm = pl.BlockSpec(memory_space=pl.ANY)
    table, padded = pl.pallas_call(
        table_body,
        out_shape=(
            jax.ShapeDtypeStruct((128, 3 * D), bf16),
            jax.ShapeDtypeStruct((128, D), bf16),
        ),
        grid=(1,),
        in_specs=[
            pl.BlockSpec((64, D), lambda n: (0, 0)),
            pl.BlockSpec((1, D, 3 * D), lambda n: (0, 0, 0)),
        ],
        out_specs=(
            pl.BlockSpec((128, 3 * D), lambda n: (0, 0)),
            pl.BlockSpec((128, D), lambda n: (0, 0)),
        ),
        name="tables",
    )(book, qkv_weight)

    n1, n0 = r1n * c1n * AREA, r0n * c0n * AREA
    natt = max(r0n * c0n, (qr + 2) * (qc + 2)) * AREA
    geo = (tr, tc, r0n, c0n, r1n, c1n, qr, qc, rr, width)
    cout = conv_weight.shape[3]
    return pl.pallas_call(
        functools.partial(body, geo),
        out_shape=jax.ShapeDtypeStruct((qr * TILE, qc * TILE, cout), bf16),
        grid=(1,),
        in_specs=[
            pl.BlockSpec((group, list_lanes), lambda n: (0, id_lanes // list_lanes), memory_space=pltpu.SMEM),
            smem, smem,
            pl.BlockSpec((id_rows, id_lanes), lambda n: (0, 0)),
            vmem, vmem, hbm, hbm, hbm,
        ],
        out_specs=pl.BlockSpec((qr * TILE, qc * TILE, cout), lambda n: (0, 0, 0)),
        scratch_shapes=[
            pltpu.VMEM((n1, 128), bf16),
            pltpu.VMEM((n1, D), bf16),
            pltpu.VMEM((n1, D), bf16),
            pltpu.VMEM((n1, D), bf16),
            pltpu.VMEM((n1, D), bf16),
            pltpu.VMEM((natt, D), bf16),
            pltpu.VMEM((n0, D), bf16),
            pltpu.VMEM((n0, D), bf16),
            pltpu.VMEM((n0, D), bf16),
            pltpu.VMEM((n0, D), bf16),
            pltpu.VMEM(((qr + 2) * TILE, (qc + 2) * TILE, D), f32),
            pltpu.VMEM((D, 3 * D), bf16),
            pltpu.VMEM((BLOCKS, D, D), bf16),
            pltpu.VMEM((3, 3, D, cout), bf16),
            pltpu.SemaphoreType.DMA((3,)),
        ],
        name="decode",
    )(everyone, place, logit_scale, window, table, padded, qkv_weight, out_weight, conv_weight)


def solution(mesh):
    in_specs = (
        P(("parts", "ha", "wa"), None),
        P(("parts", "ha"), "wa", None),
        P(),
        P(),
        P(),
        P(),
        P(),
    )
    out_specs = P(("parts", "ha"), "wa", None)
    return jax.shard_map(local, mesh=mesh, in_specs=in_specs, out_specs=out_specs, check_vma=False)
```

time: 120 us -> 48 us (0.40)
  local copies, waits for them, and re-layouts: 38.9 us -> 4.74 us
  Pallas kernels: 0 us -> 33.7 us
  starting transfers between devices: 30.5 us -> 7.39 us
  waiting for transfers between devices: 21.2 us -> 1.81 us
  other arithmetic: 14.1 us -> 0.01 us
  matrix products: 13.3 us -> 0 us
    pallas_call x0 -> x2, Pallas kernels: none -> 33.7 us  [the longest x1 31.1 us: local(): pl.pallas_call(functools.partial(body, geo), out_shape=jax.ShapeDtypeStru...]
    ppermute x10 -> x0, starting transfers between devices: 24.2 us -> none  [the longest x5 17.5 us: with_halo(): before = lax.ppermute(last, axis, up)]
    ppermute x10 -> x0, waiting for transfers between devices: 16.6 us -> none  [the longest x5 12.7 us: with_halo(): after = lax.ppermute(initial, axis, down)]
    dot_general x18 -> x0, matrix products: 9.92 us -> none  [the longest x2 2.97 us: attention_block(): jnp.dot(attended, out_block, preferred_element_type=jnp.float32)]
    reshape x9 -> x2, local copies, waits for them, and re-layouts: 10.9 us -> 1.52 us  [the longest x1 0.76 us: local(): ids = token_ids.reshape(1, rr * width)]
    slice x6 -> x0, local copies, waits for them, and re-layouts: 6.48 us -> none  [the longest x2 4.37 us: attend(): gathered[:, :, 0]]
    unnamed x30 -> x1, local copies, waits for them, and re-layouts: 7.06 us -> 0.6 us
    mul x12 -> x0, local copies, waits for them, and re-layouts: 6.4 us -> none  [the longest x8 3.56 us: normalize(): wide32 * lax.rsqrt(jnp.mean(wide32 * wide32, axis=-1, keepdims=True) + no...]
  transfers between devices with their start and end apart: 11 -> 1, of which waited for: 6 -> 1; matrix products, arithmetic and copies ran while one was open for 7% -> 4% of each run, Pallas kernels for 0% -> 5%
where the time goes in v1:
time: 48 us; the launch traced here: 47.7 us
  Pallas kernels  33.7 us (70%)
  starting transfers between devices  7.39 us (15%)
  local copies, waits for them, and re-layouts  4.74 us (10%)
  waiting for transfers between devices  1.81 us (4%)
    pallas_call x1, Pallas kernels, local(): pl.pallas_call(functools.partial(body, geo), out_shape=jax.ShapeDtypeStru...  31.1 us
    all_to_all x1, starting transfers between devices, local(): lax.all_to_all(jnp.broadcast_to(row, (group, row.shape[1])), ('ha', 'wa')...  7.39 us
    pallas_call x1, Pallas kernels, local(): pl.pallas_call(table_body, out_shape=(jax.ShapeDtypeStruct((128, 3 * D),...  2.6 us
    all_to_all x1, waiting for transfers between devices, local(): lax.all_to_all(jnp.broadcast_to(row, (group, row.shape[1])), ('ha', 'wa')...  1.81 us
    pad x1, local copies, waits for them, and re-layouts, local(): book = jnp.pad(codebook, ((0, 64 - codebook.shape[0]), (0, 0)))  1.42 us
  transfers between devices with their start and end apart: 1, of which 1 were waited for; matrix products, arithmetic and copies ran while one was open for 4% of the time, Pallas kernels for 5%

profile of v1, /device:TPU:0, one launch (start us, length us, event | category | flops | bytes accessed | tf_op | source)
XLA Modules:
  0.0 47.7 jit_solution(4304190113614599249)
XLA Ops:
  0.0 0.8 %reshape.12 = s32[1,128]{1,0:T(1,128)S(1)} reshape(s32[2,64]{1,0:T(2,128)} %param.7) | data formatting | bytes 1024 | tf_op jit(solution)/shard_map/reshape | solution.py:302
  0.8 0.8 %reshape.13 = s32[1,12]{1,0:T(1,128)S(1)} reshape(s32[1,2,6]{2,1,0:T(2,128)} %param.8) | data formatting | bytes 96 | tf_op jit(solution)/shard_map/reshape | solution.py:303
  1.5 0.6 %broadcast_in_dim.2 = s32[16,1,256]{2,1,0:T(1,128)} broadcast(s32[256]{0:T(256)S(1)} %bitcast.12), dimensions={2} | broadcast | bytes 17408 | tf_op jit(solution)/shard_map/broadcast_in_dim | solution.py:315
  2.1 7.4 %all-to-all-start = ((s32[16,1,256]{2,1,0:T(1,128)}), s32[16,1,256]{2,1,0:T(1,128)S(1)}, u32[]{:S(2)}, u32[]{:S(2)}) async-start(s32[16,1,256]{2,1,0:T(1,128)} %broadcast_in_dim.2), calls=%async_computation | async-start | bytes 32768 | tf_op jit(solution)/shard_map/all_to_all | solution.py:314
  9.6 1.4 %pad.9.book_ref = bf16[64,512]{1,0:T(8,128)(2,1)} pad(bf16[39,512]{1,0:T(8,128)(2,1)} %param.9, bf16[]{:T(256)} %constant.19.clone.1), padding=0_25x0_0 | pad | bytes 105474 | tf_op jit(solution)/shard_map/jit(_pad)/pad | solution.py:332
  11.0 2.6 %tables.1 = (bf16[128,1536]{1,0:T(8,128)(2,1)}, bf16[128,512]{1,0:T(8,128)(2,1)}) custom-call(bf16[64,512]{1,0:T(8,128)(2,1)} %pad.9.book_ref, bf16[2,512,1536]{2,1,0:T(8,128)(2,1)} %wq_hbm.1), custom_call_target="tpu_custom_call" | custom-call | tf_op jit(solution)/shard_map/tables/pallas_call | solution.py:336
  13.6 0.6 %stack.27.place_ref = s32[6]{0:T(128)} concatenate(s32[1]{0:T(128)} %bitcast.1, s32[1]{0:T(128)} %bitcast.2, s32[1]{0:T(128)} %bitcast.3, s32[1]{0:T(128)} %bitcast.4, s32[1]{0:T(128)} %bitcast.5, s32[1]{0:T(128)} %bitcast.6), dimensions={0} | concatenate | bytes 48 | tf_op jit(solution)/shard_map/stack | solution.py:326
  14.2 1.8 %all-to-all-done = s32[16,1,256]{2,1,0:T(1,128)S(1)} async-done(((s32[16,1,256]{2,1,0:T(1,128)}), s32[16,1,256]{2,1,0:T(1,128)S(1)}, u32[]{:S(2)}, u32[]{:S(2)}) %all-to-all-start) | async-done | bytes 16416 | tf_op jit(solution)/shard_map/all_to_all | solution.py:314
  16.0 0.6 %copy.10 = s32[16,1,256]{2,0,1:T(8,128)} copy(s32[16,1,256]{2,1,0:T(1,128)S(1)} %all-to-all-done) | data formatting | bytes 32768
  16.6 31.1 %decode.1 = bf16[8,16,256]{2,1,0:T(8,128)(2,1)} custom-call(s32[16,256]{1,0:T(8,128)} %bitcast.10, s32[6]{0:T(128)} %stack.27.place_ref, f32[2,8]{1,0:T(2,128)} %scale_ref.1, s32[16,256]{1,0:T(8,128)} %bitcast.11, bf16[128,1536]{1,0:T(8,128)(2,1)} %get-tuple-element.7.table_ref, bf16[128,512]{1,0:T(8,128)(2,1)} %get-tuple-element.8.book_ref, ...), custom_call_target="tpu_custom_call" | custom-call | tf_op jit(solution)/shard_map/decode/pallas_call | solution.py:358
  (1 shorter events, 0.0 us)
Async XLA Ops:
  2.1 13.8 %all-to-all-start = ((s32[16,1,256]{2,1,0:T(1,128)}), s32[16,1,256]{2,1,0:T(1,128)S(1)}, u32[]{:S(2)}, u32[]{:S(2)}) async-start(s32[16,1,256]{2,1,0:T(1,128)} %broadcast_in_dim.2), calls=%async_computation | async-start | bytes 32768 | tf_op jit(solution)/shard_map/all_to_all | solution.py:314

commit v2 on v1

v2 whole, which is shorter than its diff:
```python
import functools
import math

import jax
import jax.numpy as jnp
from jax import lax
from jax.experimental import pallas as pl
from jax.experimental.pallas import tpu as pltpu
from jax.sharding import PartitionSpec as P

D = 512
HEADS = 8
HEAD = D // HEADS
TILE = 8
AREA = TILE * TILE
NSEL = 6
BLOCKS = 2
HALF = 256
GROUP = HALF // HEAD
digit_levels = (8, 8, 8, 5, 5, 5)
digit_shift = (6, 3, 0, 9, 12, 15)
norm_eps = 1e-06
LOG2E = math.log2(math.e)
NEG = -1e30

f32 = jnp.float32
bf16 = jnp.bfloat16
i32 = jnp.int32


def mm(a, b):
    return lax.dot_general(a, b, (((1,), (0,)), ((), ())), preferred_element_type=f32)


def mm_t(a, b):
    return lax.dot_general(a, b, (((1,), (1,)), ((), ())), preferred_element_type=f32)


def span(count, size, total):
    return jnp.clip(count, 0, total - size)


def reach(starts, size, total):
    return max(min(s + size + 1, total) - max(s - 1, 0) for s in starts)


def pack_digits(ids):
    x = ids.astype(f32)
    q5 = jnp.floor((x + 0.5) * 0.2)
    q4 = jnp.floor((q5 + 0.5) * 0.2)
    q3 = jnp.floor((q4 + 0.5) * 0.2)
    return q3 + 512.0 * (q4 - 5.0 * q3) + 4096.0 * (q5 - 5.0 * q4) + 32768.0 * (x - 5.0 * q5)


def slot_tables():
    lane = lax.broadcasted_iota(i32, (1, 128), 1)
    slot = lane & 63
    shift = jnp.zeros_like(lane)
    start = jnp.zeros_like(lane)
    offset = 0
    for size, bits in zip(digit_levels, digit_shift):
        here = slot >= offset
        shift = jnp.where(here, bits, shift)
        start = jnp.where(here, offset, start)
        offset += size
    return shift, jnp.where(slot < offset, slot - start, -1)


def head_scale(x, ones_bd, floor):
    parts = []
    for half in range(D // HALF):
        piece = x[:, HALF * half : HALF * half + HALF]
        total = mm((piece * piece).astype(bf16), ones_bd)
        parts.append((piece * lax.rsqrt(total * (1.0 / HEAD) + floor)).astype(bf16))
    return jnp.concatenate(parts, axis=1)


def square_mean(x):
    return jnp.sum(x * x, axis=-1, keepdims=True) * (1.0 / D)


def attend_tile(q, starts, bias, factors, keys, values, lane_head):
    outs = []
    for g in range(D // HALF):
        cols = slice(HALF * g, HALF * g + HALF)
        qg = q[:, cols]
        q_bd = jnp.concatenate(
            [jnp.where(lane_head == h, qg, jnp.zeros_like(qg)) for h in range(GROUP)], axis=0
        )
        k = jnp.concatenate([keys[pl.ds(s, AREA), cols] for s in starts], axis=0)
        v = jnp.concatenate([values[pl.ds(s, AREA), cols] for s in starts], axis=0)
        s = mm_t(q_bd, k) + bias
        s = s - jnp.max(s, axis=-1, keepdims=True)
        p = jnp.concatenate(
            [
                jnp.exp2(s[AREA * h : AREA * h + AREA] * factors[GROUP * g + h])
                for h in range(GROUP)
            ],
            axis=0,
        )
        den = jnp.sum(p, axis=-1, keepdims=True)
        o = mm(p.astype(bf16), v) * (1.0 / den)
        r = o[:AREA]
        for h in range(1, GROUP):
            r = jnp.where(lane_head == h, o[AREA * h : AREA * h + AREA], r)
        outs.append(r)
    return jnp.concatenate(outs, axis=1).astype(bf16)


def attend_strip(q, starts, bias, factors, keys, values):
    count = q.shape[0]
    lane_head = lax.broadcasted_iota(i32, (1, D), 1) // HEAD
    q_bd = jnp.concatenate(
        [jnp.where(lane_head == h, q, jnp.zeros_like(q)) for h in range(HEADS)], axis=0
    )
    k = jnp.concatenate([keys[pl.ds(s, AREA), :] for s in starts], axis=0)
    v = jnp.concatenate([values[pl.ds(s, AREA), :] for s in starts], axis=0)
    s = mm_t(q_bd, k) + bias
    s = s - jnp.max(s, axis=-1, keepdims=True)
    p = jnp.concatenate(
        [jnp.exp2(s[count * h : count * h + count] * factors[h]) for h in range(HEADS)], axis=0
    )
    den = jnp.sum(p, axis=-1, keepdims=True)
    o = mm(p.astype(bf16), v) * (1.0 / den)
    r = o[:count]
    for h in range(1, HEADS):
        r = jnp.where(lane_head == h, o[count * h : count * h + count], r)
    return r.astype(bf16)


def block_ones():
    return (
        lax.broadcasted_iota(i32, (HALF, HALF), 0) // HEAD
        == lax.broadcasted_iota(i32, (HALF, HALF), 1) // HEAD
    ).astype(f32).astype(bf16)


def factors_of(scale_ref, layer):
    return [scale_ref[layer, h] * (LOG2E / math.sqrt(HEAD)) for h in range(HEADS)]


def rows_at(tile, count=AREA):
    return pl.ds(pl.multiple_of(tile * AREA, AREA), count)


def neighbours(geo, lists_ref, gi, gj, row0, col0, cols):
    gi = jnp.clip(gi, 0, geo.tr - 1)
    gj = jnp.clip(gj, 0, geo.tc - 1)
    owner = gi // geo.qr * (geo.tc // geo.qc) + gj // geo.qc
    at = geo.rr + gi % geo.qr * geo.qc + gj % geo.qc
    bias_tile = lax.broadcasted_iota(i32, (1, NSEL * AREA), 1) // AREA
    starts = []
    bias = jnp.zeros((1, NSEL * AREA), f32)
    for n in range(NSEL):
        number = lists_ref[owner, at, n]
        ni = gi - 1 + number // 3
        nj = gj - 1 + number % 3
        inside = (ni >= 0) & (ni < geo.tr) & (nj >= 0) & (nj < geo.tc)
        ni = jnp.where(inside, ni, gi)
        nj = jnp.where(inside, nj, gj)
        starts.append(pl.multiple_of(((ni - row0) * cols + nj - col0) * AREA, AREA))
        bias = jnp.where(bias_tile == n, jnp.where(inside, 0.0, NEG), bias)
    return starts, bias


class Geometry:
    def __init__(self, rr, width, qr, qc, down, across):
        self.rr, self.width, self.qr, self.qc = rr, width, qr, qc
        self.tr, self.tc = qr * down, qc * across
        self.sides = 2 if down % 2 == 0 else 1
        pair = qr * self.sides
        self.r0n = min(pair + 4, self.tr)
        if self.r0n % self.sides:
            self.sides, pair = 1, qr
            self.r0n = min(pair + 4, self.tr)
        self.pair = pair
        self.half = self.r0n // self.sides
        self.c0n = min(qc + 4, self.tc)
        clip = lambda at, size, total: min(max(at, 0), total - size)
        self.c1n = reach(
            [clip(n * qc - 2, self.c0n, self.tc) for n in range(across)], self.c0n, self.tc
        )
        self.r1n = reach(
            [
                clip(n * pair - 2, self.r0n, self.tr) + side * self.half
                for n in range(self.tr // pair)
                for side in range(self.sides)
            ],
            self.half,
            self.tr,
        )

    def place(self):
        ha, wa = lax.axis_index("ha"), lax.axis_index("wa")
        own_r, own_c = ha * self.qr, wa * self.qc
        side = ha % self.sides
        p0 = span(ha // self.sides * self.pair - 2, self.r0n, self.tr)
        c0 = span(own_c - 2, self.c0n, self.tc)
        r0 = p0 + side * self.half
        r1 = span(r0 - 1, self.r1n, self.tr)
        c1 = span(c0 - 1, self.c1n, self.tc)
        return own_r, own_c, side, p0, r0, c0, r1, c1


def first_body(
    geo,
    lists_ref, scale_ref, ids_ref, table_ref, book_ref, wq_hbm, wo_hbm, wc_hbm,
    out_ref, wq1_ref, wo1_ref, wc_ref,
    onehot, floors, hid0, q0, k0, v0, att, wo, sems,
):
    copies = [
        pltpu.make_async_copy(wo_hbm.at[0], wo, sems.at[0]),
        pltpu.make_async_copy(wq_hbm.at[1], wq1_ref, sems.at[1]),
        pltpu.make_async_copy(wo_hbm.at[1], wo1_ref, sems.at[2]),
        pltpu.make_async_copy(wc_hbm, wc_ref, sems.at[3]),
    ]
    for copy in copies:
        copy.start()
    own_r, own_c, side, p0, r0, c0, r1, c1 = geo.place()
    c0n, c1n, rr = geo.c0n, geo.c1n, geo.rr
    lane_head = lax.broadcasted_iota(i32, (1, HALF), 1) // HEAD
    ones_bd = block_ones()

    shift, digit = slot_tables()
    lanes = ids_ref.shape[2]
    rel = (
        lax.broadcasted_iota(i32, (AREA, lanes), 1)
        - lax.broadcasted_iota(i32, (AREA, lanes), 0) % TILE
    )
    per_tile = TILE // rr
    for i in range(geo.r1n):
        rows = []
        for n in range(per_tile):
            packed = pack_digits(ids_ref[(r1 + i) * per_tile + n])
            rows += [jnp.broadcast_to(packed[r : r + 1], (TILE, lanes)) for r in range(rr)]
        spread = jnp.concatenate(rows, axis=0)
        for j in range(c1n):
            mine = jnp.where(rel == TILE * (c1 + j), spread, 0.0)
            code = jnp.sum(mine, axis=-1, keepdims=True).astype(i32)
            hit = (lax.shift_right_logical(jnp.broadcast_to(code, (AREA, 128)), shift) & 7) == digit
            t = i * c1n + j
            onehot[AREA * t : AREA * t + AREA, :] = hit.astype(f32).astype(bf16)

    def project_keys(i, _):
        rows = rows_at(i * c1n, c1n * AREA)
        oh = onehot[rows, :]
        hid = mm(oh, book_ref[...]).astype(bf16)
        hid0[rows, :] = hid
        ms = square_mean(hid.astype(f32)) + norm_eps
        floor = norm_eps * ms
        floors[rows, :] = floor
        k0[rows, :] = head_scale(mm(oh, table_ref[:, D : 2 * D]), ones_bd, floor)
        v0[rows, :] = (mm(oh, table_ref[:, 2 * D :]) * lax.rsqrt(ms)).astype(bf16)
        return 0

    lax.fori_loop(0, geo.r1n, project_keys, 0)

    def in_window(i):
        return rows_at((r0 - r1 + i) * c1n + c0 - c1, c0n * AREA)

    def project_queries(i, _):
        rows = in_window(i)
        q = mm(onehot[rows, :], table_ref[:, :D])
        q0[rows_at(i * c0n, c0n * AREA), :] = head_scale(q, ones_bd, floors[rows, :])
        return 0

    lax.fori_loop(0, geo.half, project_queries, 0)

    factors = factors_of(scale_ref, 0)

    def attend(i, _):
        for j in range(c0n):
            starts, bias = neighbours(geo, lists_ref, r0 + i, c0 + j, r1, c1, c1n)
            here = rows_at(i * c0n + j)
            att[here, :] = attend_tile(q0[here, :], starts, bias, factors, k0, v0, lane_head)
        return 0

    lax.fori_loop(0, geo.half, attend, 0)

    copies[0].wait()

    def project_out(i, _):
        rows = rows_at(i * c0n, c0n * AREA)
        old = hid0[in_window(i), :].astype(f32)
        out_ref[rows, :] = (old + mm(att[rows, :], wo[...])).astype(bf16)
        return 0

    lax.fori_loop(0, geo.half, project_out, 0)
    for copy in copies[1:]:
        copy.wait()


STRIP = 16


def second_body(
    geo,
    lists_ref, scale_ref, own_ref, other_ref, wq, wo, wc,
    out_ref,
    hid, k1, v1, queries, q1, att, region,
):
    own_r, own_c, side, p0, r0, c0, r1, c1 = geo.place()
    c0n, qr, qc = geo.c0n, geo.qr, geo.qc
    half = geo.half * c0n
    hid[rows_at(side * half, half * AREA), :] = own_ref[...]
    if geo.sides == 2:
        hid[rows_at((1 - side) * half, half * AREA), :] = other_ref[...]
    lane_head = lax.broadcasted_iota(i32, (1, HALF), 1) // HEAD
    ones_bd = block_ones()

    def project_keys(i, _):
        rows = rows_at(i * c0n, c0n * AREA)
        h = hid[rows, :]
        ms = square_mean(h.astype(f32)) + norm_eps
        k1[rows, :] = head_scale(mm(h, wq[:, D : 2 * D]), ones_bd, norm_eps * ms)
        v1[rows, :] = (mm(h, wq[:, 2 * D :]) * lax.rsqrt(ms)).astype(bf16)
        return 0

    lax.fori_loop(0, geo.r0n, project_keys, 0)

    ring = qc + 2

    def clipped(gi, gj):
        ci = jnp.clip(gi, 0, geo.tr - 1)
        cj = jnp.clip(gj, 0, geo.tc - 1)
        return (ci - p0) * c0n + cj - c0

    whole = [(own_r + i, own_c - 1 + j) for i in range(qr) for j in range(ring)]
    strips = [(own_r - 1, own_c - 1 + j, AREA - STRIP) for j in range(ring)]
    strips += [(own_r + qr, own_c - 1 + j, 0) for j in range(ring)]
    base = len(whole) * AREA
    for n, (gi, gj) in enumerate(whole):
        queries[AREA * n : AREA * n + AREA, :] = hid[rows_at(clipped(gi, gj)), :]
    for n, (gi, gj, skip) in enumerate(strips):
        at = base + STRIP * n
        here = pl.ds(pl.multiple_of(clipped(gi, gj) * AREA + skip, STRIP), STRIP)
        queries[at : at + STRIP, :] = hid[here, :]
    h = queries[...]
    ms = square_mean(h.astype(f32)) + norm_eps
    q1[...] = head_scale(mm(h, wq[:, :D]), ones_bd, norm_eps * ms)

    factors = factors_of(scale_ref, 1)
    for n, (gi, gj) in enumerate(whole):
        starts, bias = neighbours(geo, lists_ref, gi, gj, p0, c0, c0n)
        at = slice(AREA * n, AREA * n + AREA)
        att[at, :] = attend_tile(q1[at, :], starts, bias, factors, k1, v1, lane_head)
    for n, (gi, gj, _) in enumerate(strips):
        starts, bias = neighbours(geo, lists_ref, gi, gj, p0, c0, c0n)
        at = slice(base + STRIP * n, base + STRIP * n + STRIP)
        att[at, :] = attend_strip(q1[at, :], starts, bias, factors, k1, v1)

    h = (queries[...].astype(f32) + mm(att[...], wo[...])).astype(bf16).astype(f32)
    v = h * lax.rsqrt(square_mean(h) + norm_eps)
    act = v / (1.0 + jnp.exp(-v))

    def kept(piece, gi, gj):
        inside = (gi >= 0) & (gi < geo.tr) & (gj >= 0) & (gj < geo.tc)
        return jnp.where(inside, piece, 0.0)

    for n, (gi, gj) in enumerate(whole):
        i, j = divmod(n, ring)
        tile = kept(act[AREA * n : AREA * n + AREA], gi, gj)
        for r in range(TILE):
            region[1 + TILE * i + r, TILE * j : TILE * j + TILE, :] = tile[TILE * r : TILE * r + TILE]
    for n, (gi, gj, skip) in enumerate(strips):
        i, j = divmod(n, ring)
        at = base + STRIP * n + (STRIP - TILE if skip else 0)
        row = (qr * TILE + 1) * i
        region[row, TILE * j : TILE * j + TILE, :] = kept(act[at : at + TILE], gi, gj)

    rows, cols = qr * TILE, qc * TILE
    total = jnp.zeros((rows * cols, wc.shape[-1]), f32)
    for dc in range(3):
        left = TILE - 1 + dc
        shifted = region[:, left : left + cols, :].astype(bf16)
        for dr in range(3):
            piece = shifted[dr : dr + rows].reshape(rows * cols, D)
            total = total + mm(piece, wc[dr, dc])
    out_ref[...] = total.astype(bf16).reshape(rows, cols, wc.shape[-1])


def table_body(book_ref, wq_hbm, table_ref, padded_ref, wq, sem):
    copy = pltpu.make_async_copy(wq_hbm.at[0], wq, sem)
    copy.start()
    book = jnp.concatenate(
        [book_ref[...].astype(f32), jnp.zeros((64 - book_ref.shape[0], D), f32)], axis=0
    ).astype(bf16)
    copy.wait()
    full = mm(book, wq[...])
    high = full.astype(bf16)
    low = (full - high.astype(f32)).astype(bf16)
    table_ref[...] = jnp.concatenate([high, low], axis=0)
    padded_ref[...] = jnp.concatenate([book, jnp.zeros_like(book)], axis=0)


VMEM_LIMIT = 20 << 20


def on_chip(x):
    return pltpu.with_memory_space_constraint(x, pltpu.VMEM)


def off_chip(x):
    return pltpu.with_memory_space_constraint(x, pltpu.HBM)


vmem = pl.BlockSpec(memory_space=pltpu.VMEM)
hbm = pl.BlockSpec(memory_space=pltpu.HBM)
smem = pl.BlockSpec(memory_space=pltpu.SMEM)


def local(token_ids, neighbour_lists, codebook, qkv_weight, out_weight, logit_scale, conv_weight):
    across = lax.axis_size("wa")
    down = lax.axis_size("ha")
    rr, width = token_ids.shape
    qr, qc = neighbour_lists.shape[:2]
    assert TILE % rr == 0
    geo = Geometry(rr, width, qr, qc, down, across)
    lists = neighbour_lists.reshape(qr * qc, NSEL)
    lanes = -(-width // 128) * 128
    mine = jnp.concatenate(
        [
            jnp.pad(token_ids, ((0, 0), (0, lanes - width))),
            jnp.pad(lists, ((0, 0), (0, lanes - NSEL))),
        ],
        axis=0,
    )
    everyone = lax.all_to_all(
        jnp.broadcast_to(mine, (down * across,) + mine.shape), ("ha", "wa"), 0, 0, tiled=True
    )

    table, padded = pl.pallas_call(
        table_body,
        out_shape=(pltpu.VMEM((128, 3 * D), bf16), pltpu.VMEM((128, D), bf16)),
        in_specs=[vmem, hbm],
        out_specs=(vmem, vmem),
        scratch_shapes=[pltpu.VMEM((D, 3 * D), bf16), pltpu.SemaphoreType.DMA],
        compiler_params=pltpu.CompilerParams(vmem_limit_bytes=VMEM_LIMIT),
        name="tables",
    )(codebook, off_chip(qkv_weight))

    n1 = geo.r1n * geo.c1n * AREA
    nh = geo.half * geo.c0n * AREA
    cout = conv_weight.shape[3]
    own, wq1, wo1, wc = pl.pallas_call(
        functools.partial(first_body, geo),
        out_shape=(
            pltpu.VMEM((nh, D), bf16),
            pltpu.VMEM((D, 3 * D), bf16),
            pltpu.VMEM((D, D), bf16),
            pltpu.VMEM((3, 3, D, cout), bf16),
        ),
        in_specs=[smem, smem, vmem, vmem, vmem, hbm, hbm, hbm],
        out_specs=(vmem,) * 4,
        scratch_shapes=[
            pltpu.VMEM((n1, 128), bf16),
            pltpu.VMEM((n1, 1), f32),
            pltpu.VMEM((n1, D), bf16),
            pltpu.VMEM((nh, D), bf16),
            pltpu.VMEM((n1, D), bf16),
            pltpu.VMEM((n1, D), bf16),
            pltpu.VMEM((nh, D), bf16),
            pltpu.VMEM((D, D), bf16),
            pltpu.SemaphoreType.DMA((4,)),
        ],
        compiler_params=pltpu.CompilerParams(vmem_limit_bytes=VMEM_LIMIT),
        name="first",
    )(
        everyone, logit_scale, everyone, on_chip(table), on_chip(padded),
        *map(off_chip, (qkv_weight, out_weight, conv_weight)),
    )
    other = own
    if geo.sides == 2:
        other = lax.ppermute(own, "ha", [(n, n ^ 1) for n in range(down)])

    n0 = geo.r0n * geo.c0n * AREA
    nq = qr * (qc + 2) * AREA + 2 * (qc + 2) * STRIP
    return pl.pallas_call(
        functools.partial(second_body, geo),
        out_shape=jax.ShapeDtypeStruct((qr * TILE, qc * TILE, cout), bf16),
        in_specs=[smem, smem, vmem, vmem, vmem, vmem, vmem],
        out_specs=vmem,
        scratch_shapes=[
            pltpu.VMEM((n0, D), bf16),
            pltpu.VMEM((n0, D), bf16),
            pltpu.VMEM((n0, D), bf16),
            pltpu.VMEM((nq, D), bf16),
            pltpu.VMEM((nq, D), bf16),
            pltpu.VMEM((nq, D), bf16),
            pltpu.VMEM((qr * TILE + 2, (qc + 2) * TILE, D), f32),
        ],
        compiler_params=pltpu.CompilerParams(vmem_limit_bytes=VMEM_LIMIT),
        name="second",
    )(everyone, logit_scale, *map(on_chip, (own, other, wq1, wo1, wc)))


def solution(mesh):
    in_specs = (
        P(("parts", "ha", "wa"), None),
        P(("parts", "ha"), "wa", None),
        P(),
        P(),
        P(),
        P(),
        P(),
    )
    out_specs = P(("parts", "ha"), "wa", None)
    return jax.shard_map(local, mesh=mesh, in_specs=in_specs, out_specs=out_specs, check_vma=False)
```

time: 48 us -> 38.3 us (0.80)
  Pallas kernels: 33.7 us -> 22.3 us
  waiting for transfers between devices: 1.81 us -> 6.07 us
  local copies, waits for them, and re-layouts: 4.74 us -> 1.4 us
  other arithmetic: 0.01 us -> 0.72 us
    pallas_call x2 -> x3, Pallas kernels: 33.7 us -> 22.3 us  [the longest x1 11.2 us: local(): pl.pallas_call(functools.partial(second_body, geo), out_shape=jax.ShapeDt...]
    ppermute x0 -> x1, waiting for transfers between devices: none -> 2.17 us  [local(): other = lax.ppermute(own, 'ha', [(n, n ^ 1) for n in range(down)])]
    all_to_all x1, waiting for transfers between devices: 1.81 us -> 3.9 us  [local(): lax.all_to_all(jnp.broadcast_to(mine, (down * across,) + mine.shape), ('h...]
    reshape x2 -> x0, local copies, waits for them, and re-layouts: 1.52 us -> none  [the longest x1 0.76 us: local(): ids = token_ids.reshape(1, rr * width)]
    pad x1 -> x0, local copies, waits for them, and re-layouts: 1.42 us -> none  [local(): book = jnp.pad(codebook, ((0, 64 - codebook.shape[0]), (0, 0)))]
    concatenate x1, other arithmetic: 0.01 us -> 0.72 us  [local(): jnp.concatenate([jnp.pad(token_ids, ((0, 0), (0, lanes - width))), jnp.pa...]
    another operation x1 -> x0, local copies, waits for them, and re-layouts: 0.59 us -> none  [local(): place = jnp.stack([own_r, own_c, r0, c0, r1, c1]).astype(i32)]
  transfers between devices with their start and end apart: 1 -> 2, of which waited for: 1 -> 2; matrix products, arithmetic and copies ran while one was open for 4% -> 0% of each run, Pallas kernels for 5% -> 5%
where the time goes in v2:
time: 38.3 us; the launch traced here: 38.1 us
  Pallas kernels  22.3 us (58%)
  starting transfers between devices  7.56 us (20%)
  waiting for transfers between devices  6.07 us (16%)
  local copies, waits for them, and re-layouts  1.4 us (4%)
  other arithmetic  0.72 us (2%)
    pallas_call x1, Pallas kernels, local(): pl.pallas_call(functools.partial(second_body, geo), out_shape=jax.ShapeDt...  11.2 us
    pallas_call x1, Pallas kernels, local(): pl.pallas_call(functools.partial(first_body, geo), out_shape=(pltpu.VMEM(...  9.24 us
    all_to_all x1, starting transfers between devices, local(): lax.all_to_all(jnp.broadcast_to(mine, (down * across,) + mine.shape), ('h...  7.39 us
    all_to_all x1, waiting for transfers between devices, local(): lax.all_to_all(jnp.broadcast_to(mine, (down * across,) + mine.shape), ('h...  3.9 us
    ppermute x1, waiting for transfers between devices, local(): other = lax.ppermute(own, 'ha', [(n, n ^ 1) for n in range(down)])  2.17 us
    pallas_call x1, Pallas kernels, local(): pl.pallas_call(table_body, out_shape=(pltpu.VMEM((128, 3 * D), bf16), plt...  1.81 us
    unnamed x4, local copies, waits for them, and re-layouts  0.78 us
  transfers between devices with their start and end apart: 2, of which 2 were waited for; matrix products, arithmetic and copies ran while one was open for 0% of the time, Pallas kernels for 5%

profile of v2, /device:TPU:0, one launch (start us, length us, event | category | flops | bytes accessed | tf_op | source)
XLA Modules:
  0.0 38.1 jit_solution(2077720364308751093)
XLA Ops:
  0.0 0.0 copy-start.1
  0.0 0.7 %pad_add_fusion = s32[4,128]{1,0:T(4,128)S(1)} fusion(s32[2,6]{1,0:T(2,128)} %bitcast.1, s32[2,64]{1,0:T(2,128)} %param.7), kind=kLoop, calls=%fused_computation | loop fusion | flops 512 | bytes 2608 | tf_op jit(solution)/shard_map/concatenate | solution.py:421
  0.7 0.6 %broadcast_in_dim.3 = s32[16,4,128]{2,1,0:T(4,128)} broadcast(s32[4,128]{1,0:T(4,128)S(1)} %pad_add_fusion), dimensions={1,2} | broadcast | bytes 34816 | tf_op jit(solution)/shard_map/broadcast_in_dim | solution.py:429
  1.3 7.4 %all-to-all-start = ((s32[16,4,128]{2,1,0:T(4,128)}), s32[16,4,128]{2,1,0:T(4,128)S(1)}, u32[]{:S(2)}, u32[]{:S(2)}) async-start(s32[16,4,128]{2,1,0:T(4,128)} %broadcast_in_dim.3), calls=%async_computation | async-start | bytes 65536 | tf_op jit(solution)/shard_map/all_to_all | solution.py:428
  8.7 0.0 copy-start
  8.7 0.8 %copy-done = bf16[39,512]{1,0:T(8,128)(2,1)S(1)} copy-done((bf16[39,512]{1,0:T(8,128)(2,1)S(1)}, bf16[39,512]{1,0:T(8,128)(2,1)}, u32[]{:S(2)}) %copy-start) | copy-done | bytes 39960
  9.5 1.8 %tables.1 = (bf16[128,1536]{1,0:T(8,128)(2,1)S(1)}, bf16[128,512]{1,0:T(8,128)(2,1)S(1)}) custom-call(bf16[39,512]{1,0:T(8,128)(2,1)S(1)} %copy-done, bf16[2,512,1536]{2,1,0:T(8,128)(2,1)} %wq_hbm.3), custom_call_target="tpu_custom_call" | custom-call | tf_op jit(solution)/shard_map/tables/pallas_call | solution.py:432
  11.3 3.9 %all-to-all-done.lists_ref.ids_ref = s32[16,4,128]{2,1,0:T(4,128)S(1)} async-done(((s32[16,4,128]{2,1,0:T(4,128)}), s32[16,4,128]{2,1,0:T(4,128)S(1)}, u32[]{:S(2)}, u32[]{:S(2)}) %all-to-all-start) | async-done | bytes 32800 | tf_op jit(solution)/shard_map/all_to_all | solution.py:428
  15.2 0.0 copy-done.1
  15.2 9.2 %first.1 = (bf16[768,512]{1,0:T(8,128)(2,1)S(1)}, bf16[512,1536]{1,0:T(8,128)(2,1)S(1)}, bf16[512,512]{1,0:T(8,128)(2,1)S(1)}, bf16[3,3,512,256]{3,2,1,0:T(8,128)(2,1)S(1)}) custom-call(s32[16,4,128]{2,1,0:T(4,128)S(1)} %all-to-all-done.lists_ref.ids_ref, f32[2,8]{1,0:T(2,128)S(1)} %copy-done.1, s32[16,4,128]{2,1,0:T(4,128)S(1)} %all-to-all-done.lists_ref.ids_ref, ...), custom_call_target="tpu_custom_call" | custom-call | tf_op jit(solution)/shard_map/first/pallas_call | solution.py:445
  24.5 0.2 collective-permute-start
  24.7 2.2 %collective-permute-done.other_ref = bf16[768,512]{1,0:T(8,128)(2,1)S(1)} collective-permute-done((bf16[768,512]{1,0:T(8,128)(2,1)S(1)}, bf16[768,512]{1,0:T(8,128)(2,1)S(1)}, u32[]{:S(2)}, u32[]{:S(2)}) %collective-permute-start) | collective-permute-done | bytes 786464 | tf_op jit(solution)/shard_map/ppermute | solution.py:474
  26.8 11.2 %second.1 = bf16[8,16,256]{2,1,0:T(8,128)(2,1)} custom-call(s32[16,4,128]{2,1,0:T(4,128)S(1)} %all-to-all-done.lists_ref.ids_ref, f32[2,8]{1,0:T(2,128)S(1)} %copy-done.1, bf16[768,512]{1,0:T(8,128)(2,1)S(1)} %get-tuple-element.13.own_ref, bf16[768,512]{1,0:T(8,128)(2,1)S(1)} %collective-permute-done.other_ref, bf16[512,1536]{1,0:T(8,128)(2,1)S(1)} %get-tuple-element.14.wq, ...), custom_call_target="tpu_custom_call" | custom-call | tf_op jit(solution)/shard_map/second/pallas_call | solution.py:478
Async XLA Ops:
  0.0 15.2 %copy-start.1 = (f32[2,8]{1,0:T(2,128)S(1)}, f32[2,8]{1,0:T(2,128)}, u32[]{:S(2)}) copy-start(f32[2,8]{1,0:T(2,128)} %scale_ref.3) | copy-start | bytes 196
  1.3 13.9 %all-to-all-start = ((s32[16,4,128]{2,1,0:T(4,128)}), s32[16,4,128]{2,1,0:T(4,128)S(1)}, u32[]{:S(2)}, u32[]{:S(2)}) async-start(s32[16,4,128]{2,1,0:T(4,128)} %broadcast_in_dim.3), calls=%async_computation | async-start | bytes 65536 | tf_op jit(solution)/shard_map/all_to_all | solution.py:428
  8.7 0.8 %copy-start = (bf16[39,512]{1,0:T(8,128)(2,1)S(1)}, bf16[39,512]{1,0:T(8,128)(2,1)}, u32[]{:S(2)}) copy-start(bf16[39,512]{1,0:T(8,128)(2,1)} %book_ref.1) | copy-start | bytes 119812
  24.5 2.4 %collective-permute-start = (bf16[768,512]{1,0:T(8,128)(2,1)S(1)}, bf16[768,512]{1,0:T(8,128)(2,1)S(1)}, u32[]{:S(2)}, u32[]{:S(2)}) collective-permute-start(bf16[768,512]{1,0:T(8,128)(2,1)S(1)} %get-tuple-element.13.own_ref), channel_id=1, source_target_pairs={{0,4},{4,0},{8,12},{12,8},{1,5},{5,1},{9,13},{13,9},{2,6},{6,2},{1... | collective-permute-start | bytes 2359304 | tf_op jit(solution)/shard_map/ppermute | solution.py:474

commit v3 on v2

--- a/solution.py
+++ b/solution.py
@@ -147,7 +147,7 @@
     gi = jnp.clip(gi, 0, geo.tr - 1)
     gj = jnp.clip(gj, 0, geo.tc - 1)
     owner = gi // geo.qr * (geo.tc // geo.qc) + gj // geo.qc
-    at = geo.rr + gi % geo.qr * geo.qc + gj % geo.qc
+    at = gi % geo.qr * geo.qc + gj % geo.qc
     bias_tile = lax.broadcasted_iota(i32, (1, NSEL * AREA), 1) // AREA
     starts = []
     bias = jnp.zeros((1, NSEL * AREA), f32)
@@ -204,15 +204,17 @@
 
 def first_body(
     geo,
-    lists_ref, scale_ref, ids_ref, table_ref, book_ref, wq_hbm, wo_hbm, wc_hbm,
+    scale_hbm, ids_ref, table_ref, book_ref, wq_hbm, wo_hbm, wc_hbm,
     out_ref, wq1_ref, wo1_ref, wc_ref,
-    onehot, floors, hid0, q0, k0, v0, att, wo, sems,
+    lists_ref, scale_ref, onehot, floors, hid0, q0, k0, v0, att, wo, sems,
 ):
     copies = [
-        pltpu.make_async_copy(wo_hbm.at[0], wo, sems.at[0]),
-        pltpu.make_async_copy(wq_hbm.at[1], wq1_ref, sems.at[1]),
-        pltpu.make_async_copy(wo_hbm.at[1], wo1_ref, sems.at[2]),
-        pltpu.make_async_copy(wc_hbm, wc_ref, sems.at[3]),
+        pltpu.make_async_copy(ids_ref.at[:, pl.ds(geo.rr, geo.qr * geo.qc), :], lists_ref, sems.at[0]),
+        pltpu.make_async_copy(scale_hbm, scale_ref, sems.at[1]),
+        pltpu.make_async_copy(wo_hbm.at[0], wo, sems.at[2]),
+        pltpu.make_async_copy(wq_hbm.at[1], wq1_ref, sems.at[3]),
+        pltpu.make_async_copy(wo_hbm.at[1], wo1_ref, sems.at[4]),
+        pltpu.make_async_copy(wc_hbm, wc_ref, sems.at[5]),
     ]
     for copy in copies:
         copy.start()
@@ -266,6 +268,8 @@
 
     lax.fori_loop(0, geo.half, project_queries, 0)
 
+    copies[0].wait()
+    copies[1].wait()
     factors = factors_of(scale_ref, 0)
 
     def attend(i, _):
@@ -277,7 +281,7 @@
 
     lax.fori_loop(0, geo.half, attend, 0)
 
-    copies[0].wait()
+    copies[2].wait()
 
     def project_out(i, _):
         rows = rows_at(i * c0n, c0n * AREA)
@@ -286,8 +290,34 @@
         return 0
 
     lax.fori_loop(0, geo.half, project_out, 0)
-    for copy in copies[1:]:
+    for copy in copies[3:]:
         copy.wait()
+
+
+def layer1_keys(hid, wq, ones_bd, rows, k1, v1):
+    h = hid[rows, :]
+    ms = square_mean(h.astype(f32)) + norm_eps
+    k1[rows, :] = head_scale(mm(h, wq[:, D : 2 * D]), ones_bd, norm_eps * ms)
+    v1[rows, :] = (mm(h, wq[:, 2 * D :]) * lax.rsqrt(ms)).astype(bf16)
+
+
+def half_keys(geo, source, side, wq, hid, k1, v1):
+    ones_bd = block_ones()
+    step = geo.c0n
+    first = side * geo.half
+
+    def one(i, _):
+        rows = rows_at((first + i) * step, step * AREA)
+        hid[rows, :] = source[rows_at(i * step, step * AREA), :]
+        layer1_keys(hid, wq, ones_bd, rows, k1, v1)
+        return 0
+
+    lax.fori_loop(0, geo.half, one, 0)
+
+
+def own_keys_body(geo, own_ref, wq, hid, k1, v1):
+    side = geo.place()[2]
+    half_keys(geo, own_ref, side, wq, hid, k1, v1)
 
 
 STRIP = 16
@@ -295,28 +325,22 @@
 
 def second_body(
     geo,
-    lists_ref, scale_ref, own_ref, other_ref, wq, wo, wc,
-    out_ref,
-    hid, k1, v1, queries, q1, att, region,
+    scale_hbm, ids_ref, other_ref, wq, wo, wc, hid_in, k1_in, v1_in,
+    out_ref, hid, k1, v1,
+    lists_ref, scale_ref, queries, q1, att, region, sems,
 ):
+    copies = [
+        pltpu.make_async_copy(ids_ref.at[:, pl.ds(geo.rr, geo.qr * geo.qc), :], lists_ref, sems.at[0]),
+        pltpu.make_async_copy(scale_hbm, scale_ref, sems.at[1]),
+    ]
+    for copy in copies:
+        copy.start()
     own_r, own_c, side, p0, r0, c0, r1, c1 = geo.place()
     c0n, qr, qc = geo.c0n, geo.qr, geo.qc
-    half = geo.half * c0n
-    hid[rows_at(side * half, half * AREA), :] = own_ref[...]
-    if geo.sides == 2:
-        hid[rows_at((1 - side) * half, half * AREA), :] = other_ref[...]
     lane_head = lax.broadcasted_iota(i32, (1, HALF), 1) // HEAD
     ones_bd = block_ones()
-
-    def project_keys(i, _):
-        rows = rows_at(i * c0n, c0n * AREA)
-        h = hid[rows, :]
-        ms = square_mean(h.astype(f32)) + norm_eps
-        k1[rows, :] = head_scale(mm(h, wq[:, D : 2 * D]), ones_bd, norm_eps * ms)
-        v1[rows, :] = (mm(h, wq[:, 2 * D :]) * lax.rsqrt(ms)).astype(bf16)
-        return 0
-
-    lax.fori_loop(0, geo.r0n, project_keys, 0)
+    if geo.sides == 2:
+        half_keys(geo, other_ref, 1 - side, wq, hid, k1, v1)
 
     ring = qc + 2
 
@@ -339,6 +363,8 @@
     ms = square_mean(h.astype(f32)) + norm_eps
     q1[...] = head_scale(mm(h, wq[:, :D]), ones_bd, norm_eps * ms)
 
+    for copy in copies:
+        copy.wait()
     factors = factors_of(scale_ref, 1)
     for n, (gi, gj) in enumerate(whole):
         starts, bias = neighbours(geo, lists_ref, gi, gj, p0, c0, c0n)
@@ -406,7 +432,6 @@
 
 vmem = pl.BlockSpec(memory_space=pltpu.VMEM)
 hbm = pl.BlockSpec(memory_space=pltpu.HBM)
-smem = pl.BlockSpec(memory_space=pltpu.SMEM)
 
 
 def local(token_ids, neighbour_lists, codebook, qkv_weight, out_weight, logit_scale, conv_weight):
@@ -418,16 +443,14 @@
     geo = Geometry(rr, width, qr, qc, down, across)
     lists = neighbour_lists.reshape(qr * qc, NSEL)
     lanes = -(-width // 128) * 128
-    mine = jnp.concatenate(
-        [
-            jnp.pad(token_ids, ((0, 0), (0, lanes - width))),
-            jnp.pad(lists, ((0, 0), (0, lanes - NSEL))),
-        ],
-        axis=0,
+    group = down * across
+    count = rr + qr * qc
+    mine = jnp.pad(
+        jnp.broadcast_to(token_ids, (group, rr, width)), ((0, 0), (0, count - rr), (0, lanes - width))
+    ) + jnp.pad(
+        jnp.broadcast_to(lists, (group, qr * qc, NSEL)), ((0, 0), (rr, 0), (0, lanes - NSEL))
     )
-    everyone = lax.all_to_all(
-        jnp.broadcast_to(mine, (down * across,) + mine.shape), ("ha", "wa"), 0, 0, tiled=True
-    )
+    everyone = lax.all_to_all(mine, ("ha", "wa"), 0, 0, tiled=True)
 
     table, padded = pl.pallas_call(
         table_body,
@@ -439,6 +462,10 @@
         name="tables",
     )(codebook, off_chip(qkv_weight))
 
+    scalars = [
+        pltpu.SMEM((down * across, qr * qc, lanes), i32),
+        pltpu.SMEM(logit_scale.shape, f32),
+    ]
     n1 = geo.r1n * geo.c1n * AREA
     nh = geo.half * geo.c0n * AREA
     cout = conv_weight.shape[3]
@@ -450,9 +477,10 @@
             pltpu.VMEM((D, D), bf16),
             pltpu.VMEM((3, 3, D, cout), bf16),
         ),
-        in_specs=[smem, smem, vmem, vmem, vmem, hbm, hbm, hbm],
+        in_specs=[hbm, vmem, vmem, vmem, hbm, hbm, hbm],
         out_specs=(vmem,) * 4,
         scratch_shapes=[
+            *scalars,
             pltpu.VMEM((n1, 128), bf16),
             pltpu.VMEM((n1, 1), f32),
             pltpu.VMEM((n1, D), bf16),
@@ -461,12 +489,12 @@
             pltpu.VMEM((n1, D), bf16),
             pltpu.VMEM((nh, D), bf16),
             pltpu.VMEM((D, D), bf16),
-            pltpu.SemaphoreType.DMA((4,)),
+            pltpu.SemaphoreType.DMA((6,)),
         ],
         compiler_params=pltpu.CompilerParams(vmem_limit_bytes=VMEM_LIMIT),
         name="first",
     )(
-        everyone, logit_scale, everyone, on_chip(table), on_chip(padded),
+        off_chip(logit_scale), on_chip(everyone), on_chip(table), on_chip(padded),
         *map(off_chip, (qkv_weight, out_weight, conv_weight)),
     )
     other = own
@@ -475,23 +503,36 @@
 
     n0 = geo.r0n * geo.c0n * AREA
     nq = qr * (qc + 2) * AREA + 2 * (qc + 2) * STRIP
+    window = pltpu.VMEM((n0, D), bf16)
+    wq1, wo1, wc = map(on_chip, (wq1, wo1, wc))
+    state = pl.pallas_call(
+        functools.partial(own_keys_body, geo),
+        out_shape=(window,) * 3,
+        in_specs=[vmem, vmem],
+        out_specs=(vmem,) * 3,
+        compiler_params=pltpu.CompilerParams(vmem_limit_bytes=VMEM_LIMIT),
+        name="own_keys",
+    )(on_chip(own), wq1)
     return pl.pallas_call(
         functools.partial(second_body, geo),
-        out_shape=jax.ShapeDtypeStruct((qr * TILE, qc * TILE, cout), bf16),
-        in_specs=[smem, smem, vmem, vmem, vmem, vmem, vmem],
-        out_specs=vmem,
+        out_shape=(jax.ShapeDtypeStruct((qr * TILE, qc * TILE, cout), bf16),) + (window,) * 3,
+        in_specs=[hbm] + [vmem] * 8,
+        out_specs=(vmem,) * 4,
+        input_output_aliases={6: 1, 7: 2, 8: 3},
         scratch_shapes=[
-            pltpu.VMEM((n0, D), bf16),
-            pltpu.VMEM((n0, D), bf16),
-            pltpu.VMEM((n0, D), bf16),
+            *scalars,
             pltpu.VMEM((nq, D), bf16),
             pltpu.VMEM((nq, D), bf16),
             pltpu.VMEM((nq, D), bf16),
             pltpu.VMEM((qr * TILE + 2, (qc + 2) * TILE, D), f32),
+            pltpu.SemaphoreType.DMA((2,)),
         ],
         compiler_params=pltpu.CompilerParams(vmem_limit_bytes=VMEM_LIMIT),
         name="second",
-    )(everyone, logit_scale, *map(on_chip, (own, other, wq1, wo1, wc)))
+    )(
+        off_chip(logit_scale), on_chip(everyone), on_chip(other), wq1, wo1, wc,
+        *map(on_chip, state),
+    )[0]
 
 
 def solution(mesh):

time: 38.3 us -> 34.7 us (0.906)
  Pallas kernels: 22.3 us -> 20.2 us
  waiting for transfers between devices: 6.07 us -> 4.52 us
    ppermute x1, waiting for transfers between devices: 2.17 us -> 0.62 us  [local(): other = lax.ppermute(own, 'ha', [(n, n ^ 1) for n in range(down)])]
    pallas_call x1, Pallas kernels: 9.24 us -> 8.22 us  [local(): pl.pallas_call(functools.partial(first_body, geo), out_shape=(pltpu.VMEM(...]
    pallas_call x1 -> x2, Pallas kernels: 11.2 us -> 10.2 us  [the longest x1 8.67 us: local(): pl.pallas_call(functools.partial(second_body, geo), out_shape=(jax.ShapeD...]
    concatenate x1 -> x0, other arithmetic: 0.72 us -> none  [local(): jnp.concatenate([jnp.pad(token_ids, ((0, 0), (0, lanes - width))), jnp.pa...]
    add x0 -> x1, other arithmetic: none -> 0.7 us  [local(): jnp.pad(jnp.broadcast_to(token_ids, (group, rr, width)), ((0, 0), (0, cou...]
    broadcast_in_dim x1 -> x0, local copies, waits for them, and re-layouts: 0.62 us -> none  [local(): jnp.broadcast_to(mine, (down * across,) + mine.shape)]
    pad x0 -> x1, local copies, waits for them, and re-layouts: none -> 0.62 us  [local(): jnp.pad(jnp.broadcast_to(token_ids, (group, rr, width)), ((0, 0), (0, cou...]
    unnamed x4 -> x2, local copies, waits for them, and re-layouts: 0.78 us -> 0.77 us
  transfers between devices with their start and end apart: 2 -> 2, of which waited for: 2 -> 2; matrix products, arithmetic and copies ran while one was open for 0% -> 0% of each run, Pallas kernels for 5% -> 10%
where the time goes in v3:
time: 34.7 us; the launch traced here: 34.5 us
  Pallas kernels  20.2 us (58%)
  starting transfers between devices  7.56 us (22%)
  waiting for transfers between devices  4.52 us (13%)
  local copies, waits for them, and re-layouts  1.39 us (4%)
  other arithmetic  0.7 us (2%)
    pallas_call x1, Pallas kernels, local(): pl.pallas_call(functools.partial(second_body, geo), out_shape=(jax.ShapeD...  8.67 us
    pallas_call x1, Pallas kernels, local(): pl.pallas_call(functools.partial(first_body, geo), out_shape=(pltpu.VMEM(...  8.22 us
    all_to_all x1, starting transfers between devices, local(): everyone = lax.all_to_all(mine, ('ha', 'wa'), 0, 0, tiled=True)  7.39 us
    all_to_all x1, waiting for transfers between devices, local(): everyone = lax.all_to_all(mine, ('ha', 'wa'), 0, 0, tiled=True)  3.9 us
    pallas_call x1, Pallas kernels, local(): pl.pallas_call(table_body, out_shape=(pltpu.VMEM((128, 3 * D), bf16), plt...  1.81 us
    pallas_call x1, Pallas kernels, local(): pl.pallas_call(functools.partial(own_keys_body, geo), out_shape=(window,)...  1.54 us
    unnamed x2, local copies, waits for them, and re-layouts  0.77 us
    add x1, other arithmetic, local(): jnp.pad(jnp.broadcast_to(token_ids, (group, rr, width)), ((0, 0), (0, cou...  0.7 us
  transfers between devices with their start and end apart: 2, of which 2 were waited for; matrix products, arithmetic and copies ran while one was open for 0% of the time, Pallas kernels for 10%

profile of v3, /device:TPU:0, one launch (start us, length us, event | category | flops | bytes accessed | tf_op | source)
XLA Modules:
  0.0 34.5 jit_solution(2082196386211462613)
XLA Ops:
  0.0 0.7 %pad_add_fusion = s32[4,128]{1,0:T(4,128)S(1)} fusion(s32[2,6]{1,0:T(2,128)} %bitcast.1, s32[2,64]{1,0:T(2,128)} %param.7), kind=kLoop, calls=%fused_computation | loop fusion | flops 512 | bytes 2608 | tf_op jit(solution)/shard_map/add | solution.py:448
  0.7 0.6 %pad.12 = s32[16,4,128]{2,1,0:T(4,128)} broadcast(s32[4,128]{1,0:T(4,128)S(1)} %pad_add_fusion), dimensions={1,2} | broadcast | bytes 34816 | tf_op jit(solution)/shard_map/jit(_pad)/pad | solution.py:448
  1.3 7.4 %all-to-all-start = ((s32[16,4,128]{2,1,0:T(4,128)}), s32[16,4,128]{2,1,0:T(4,128)S(1)}, u32[]{:S(2)}, u32[]{:S(2)}) async-start(s32[16,4,128]{2,1,0:T(4,128)} %pad.12), calls=%async_computation | async-start | bytes 65536 | tf_op jit(solution)/shard_map/all_to_all | solution.py:453
  8.7 0.0 copy-start
  8.7 0.8 %copy-done = bf16[39,512]{1,0:T(8,128)(2,1)S(1)} copy-done((bf16[39,512]{1,0:T(8,128)(2,1)S(1)}, bf16[39,512]{1,0:T(8,128)(2,1)}, u32[]{:S(2)}) %copy-start) | copy-done | bytes 39960
  9.5 1.8 %tables.1 = (bf16[128,1536]{1,0:T(8,128)(2,1)S(1)}, bf16[128,512]{1,0:T(8,128)(2,1)S(1)}) custom-call(bf16[39,512]{1,0:T(8,128)(2,1)S(1)} %copy-done, bf16[2,512,1536]{2,1,0:T(8,128)(2,1)} %wq_hbm.3), custom_call_target="tpu_custom_call" | custom-call | tf_op jit(solution)/shard_map/tables/pallas_call | solution.py:455
  11.3 3.9 %all-to-all-done.ids_ref = s32[16,4,128]{2,1,0:T(4,128)S(1)} async-done(((s32[16,4,128]{2,1,0:T(4,128)}), s32[16,4,128]{2,1,0:T(4,128)S(1)}, u32[]{:S(2)}, u32[]{:S(2)}) %all-to-all-start) | async-done | bytes 32800 | tf_op jit(solution)/shard_map/all_to_all | solution.py:453
  15.2 8.2 %first.1 = (bf16[768,512]{1,0:T(8,128)(2,1)S(1)}, bf16[512,1536]{1,0:T(8,128)(2,1)S(1)}, bf16[512,512]{1,0:T(8,128)(2,1)S(1)}, bf16[3,3,512,256]{3,2,1,0:T(8,128)(2,1)S(1)}) custom-call(f32[2,8]{1,0:T(2,128)} %scale_hbm.3, s32[16,4,128]{2,1,0:T(4,128)S(1)} %all-to-all-done.ids_ref, bf16[128,1536]{1,0:T(8,128)(2,1)S(1)} %get-tuple-element.15.table_ref, ...), custom_call_target="tpu_custom_call" | custom-call | tf_op jit(solution)/shard_map/first/pallas_call | solution.py:472
  23.4 0.2 collective-permute-start
  23.6 1.5 %own_keys.1 = (bf16[1536,512]{1,0:T(8,128)(2,1)S(1)}, bf16[1536,512]{1,0:T(8,128)(2,1)S(1)}, bf16[1536,512]{1,0:T(8,128)(2,1)S(1)}) custom-call(bf16[768,512]{1,0:T(8,128)(2,1)S(1)} %get-tuple-element.17.own_ref, bf16[512,1536]{1,0:T(8,128)(2,1)S(1)} %get-tuple-element.18.wq), custom_call_target="tpu_custom_call" | custom-call | tf_op jit(solution)/shard_map/own_keys/pallas_call | solution.py:508
  25.2 0.6 %collective-permute-done.other_ref = bf16[768,512]{1,0:T(8,128)(2,1)S(1)} collective-permute-done((bf16[768,512]{1,0:T(8,128)(2,1)S(1)}, bf16[768,512]{1,0:T(8,128)(2,1)S(1)}, u32[]{:S(2)}, u32[]{:S(2)}) %collective-permute-start) | collective-permute-done | bytes 786464 | tf_op jit(solution)/shard_map/ppermute | solution.py:502
  25.8 8.7 %second.1 = (bf16[8,16,256]{2,1,0:T(8,128)(2,1)}, bf16[1536,512]{1,0:T(8,128)(2,1)S(1)}, bf16[1536,512]{1,0:T(8,128)(2,1)S(1)}, bf16[1536,512]{1,0:T(8,128)(2,1)S(1)}) custom-call(f32[2,8]{1,0:T(2,128)} %scale_hbm.3, s32[16,4,128]{2,1,0:T(4,128)S(1)} %all-to-all-done.ids_ref, ...), custom_call_target="tpu_custom_call", output_to_operand_aliasing={{1}: (6, {}), {2}: (7, {}), {3}: (8, {})} | custom-call | tf_op jit(solution)/shard_map/second/pallas_call | solution.py:516
Async XLA Ops:
  1.3 13.9 %all-to-all-start = ((s32[16,4,128]{2,1,0:T(4,128)}), s32[16,4,128]{2,1,0:T(4,128)S(1)}, u32[]{:S(2)}, u32[]{:S(2)}) async-start(s32[16,4,128]{2,1,0:T(4,128)} %pad.12), calls=%async_computation | async-start | bytes 65536 | tf_op jit(solution)/shard_map/all_to_all | solution.py:453
  8.7 0.8 %copy-start = (bf16[39,512]{1,0:T(8,128)(2,1)S(1)}, bf16[39,512]{1,0:T(8,128)(2,1)}, u32[]{:S(2)}) copy-start(bf16[39,512]{1,0:T(8,128)(2,1)} %book_ref.1) | copy-start | bytes 119812
  23.4 2.4 %collective-permute-start = (bf16[768,512]{1,0:T(8,128)(2,1)S(1)}, bf16[768,512]{1,0:T(8,128)(2,1)S(1)}, u32[]{:S(2)}, u32[]{:S(2)}) collective-permute-start(bf16[768,512]{1,0:T(8,128)(2,1)S(1)} %get-tuple-element.17.own_ref), channel_id=1, source_target_pairs={{0,4},{4,0},{8,12},{12,8},{1,5},{5,1},{9,13},{13,9},{2,6},{6,2},{1... | collective-permute-start | bytes 2359304 | tf_op jit(solution)/shard_map/ppermute | solution.py:502

commit v4 on v3

--- a/solution.py
+++ b/solution.py
@@ -255,7 +255,8 @@
         v0[rows, :] = (mm(oh, table_ref[:, 2 * D :]) * lax.rsqrt(ms)).astype(bf16)
         return 0
 
-    lax.fori_loop(0, geo.r1n, project_keys, 0)
+    for i in range(geo.r1n):
+        project_keys(i, 0)
 
     def in_window(i):
         return rows_at((r0 - r1 + i) * c1n + c0 - c1, c0n * AREA)
@@ -266,7 +267,8 @@
         q0[rows_at(i * c0n, c0n * AREA), :] = head_scale(q, ones_bd, floors[rows, :])
         return 0
 
-    lax.fori_loop(0, geo.half, project_queries, 0)
+    for i in range(geo.half):
+        project_queries(i, 0)
 
     copies[0].wait()
     copies[1].wait()
@@ -279,7 +281,8 @@
             att[here, :] = attend_tile(q0[here, :], starts, bias, factors, k0, v0, lane_head)
         return 0
 
-    lax.fori_loop(0, geo.half, attend, 0)
+    for i in range(geo.half):
+        attend(i, 0)
 
     copies[2].wait()
 
@@ -289,7 +292,8 @@
         out_ref[rows, :] = (old + mm(att[rows, :], wo[...])).astype(bf16)
         return 0
 
-    lax.fori_loop(0, geo.half, project_out, 0)
+    for i in range(geo.half):
+        project_out(i, 0)
     for copy in copies[3:]:
         copy.wait()
 
@@ -301,7 +305,7 @@
     v1[rows, :] = (mm(h, wq[:, 2 * D :]) * lax.rsqrt(ms)).astype(bf16)
 
 
-def half_keys(geo, source, side, wq, hid, k1, v1):
+def half_keys(geo, source, side, wq, hid, k1, v1, unroll):
     ones_bd = block_ones()
     step = geo.c0n
     first = side * geo.half
@@ -312,12 +316,16 @@
         layer1_keys(hid, wq, ones_bd, rows, k1, v1)
         return 0
 
-    lax.fori_loop(0, geo.half, one, 0)
+    if unroll:
+        for i in range(geo.half):
+            one(i, 0)
+    else:
+        lax.fori_loop(0, geo.half, one, 0)
 
 
 def own_keys_body(geo, own_ref, wq, hid, k1, v1):
     side = geo.place()[2]
-    half_keys(geo, own_ref, side, wq, hid, k1, v1)
+    half_keys(geo, own_ref, side, wq, hid, k1, v1, True)
 
 
 STRIP = 16
@@ -340,7 +348,7 @@
     lane_head = lax.broadcasted_iota(i32, (1, HALF), 1) // HEAD
     ones_bd = block_ones()
     if geo.sides == 2:
-        half_keys(geo, other_ref, 1 - side, wq, hid, k1, v1)
+        half_keys(geo, other_ref, 1 - side, wq, hid, k1, v1, False)
 
     ring = qc + 2
 

time: 34.7 us -> 33.9 us (0.977)
  Pallas kernels: 20.2 us -> 19.1 us
    pallas_call x1, Pallas kernels: 8.22 us -> 7.09 us  [local(): pl.pallas_call(functools.partial(first_body, geo), out_shape=(pltpu.VMEM(...]
  transfers between devices with their start and end apart: 2 -> 2, of which waited for: 2 -> 2; matrix products, arithmetic and copies ran while one was open for 0% -> 0% of each run, Pallas kernels for 10% -> 9%
where the time goes in v4:
time: 33.9 us; the launch traced here: 33.7 us
  Pallas kernels  19.1 us (56%)
  starting transfers between devices  7.57 us (22%)
  waiting for transfers between devices  4.74 us (14%)
  local copies, waits for them, and re-layouts  1.39 us (4%)
  other arithmetic  0.7 us (2%)
    pallas_call x1, Pallas kernels, local(): pl.pallas_call(functools.partial(second_body, geo), out_shape=(jax.ShapeD...  8.83 us
    all_to_all x1, starting transfers between devices, local(): everyone = lax.all_to_all(mine, ('ha', 'wa'), 0, 0, tiled=True)  7.39 us
    pallas_call x1, Pallas kernels, local(): pl.pallas_call(functools.partial(first_body, geo), out_shape=(pltpu.VMEM(...  7.09 us
    all_to_all x1, waiting for transfers between devices, local(): everyone = lax.all_to_all(mine, ('ha', 'wa'), 0, 0, tiled=True)  3.9 us
    pallas_call x1, Pallas kernels, local(): pl.pallas_call(table_body, out_shape=(pltpu.VMEM((128, 3 * D), bf16), plt...  1.81 us
    pallas_call x1, Pallas kernels, local(): pl.pallas_call(functools.partial(own_keys_body, geo), out_shape=(window,)...  1.33 us
    ppermute x1, waiting for transfers between devices, local(): other = lax.ppermute(own, 'ha', [(n, n ^ 1) for n in range(down)])  0.83 us
    unnamed x2, local copies, waits for them, and re-layouts  0.77 us
  transfers between devices with their start and end apart: 2, of which 2 were waited for; matrix products, arithmetic and copies ran while one was open for 0% of the time, Pallas kernels for 9%

profile of v4, /device:TPU:0, one launch (start us, length us, event | category | flops | bytes accessed | tf_op | source)
XLA Modules:
  0.0 33.7 jit_solution(14900376450987844000)
XLA Ops:
  0.0 0.7 %pad_add_fusion = s32[4,128]{1,0:T(4,128)S(1)} fusion(s32[2,6]{1,0:T(2,128)} %bitcast.1, s32[2,64]{1,0:T(2,128)} %param.7), kind=kLoop, calls=%fused_computation | loop fusion | flops 512 | bytes 2608 | tf_op jit(solution)/shard_map/add | solution.py:456
  0.7 0.6 %pad.12 = s32[16,4,128]{2,1,0:T(4,128)} broadcast(s32[4,128]{1,0:T(4,128)S(1)} %pad_add_fusion), dimensions={1,2} | broadcast | bytes 34816 | tf_op jit(solution)/shard_map/jit(_pad)/pad | solution.py:456
  1.3 7.4 %all-to-all-start = ((s32[16,4,128]{2,1,0:T(4,128)}), s32[16,4,128]{2,1,0:T(4,128)S(1)}, u32[]{:S(2)}, u32[]{:S(2)}) async-start(s32[16,4,128]{2,1,0:T(4,128)} %pad.12), calls=%async_computation | async-start | bytes 65536 | tf_op jit(solution)/shard_map/all_to_all | solution.py:461
  8.7 0.0 copy-start
  8.7 0.8 %copy-done = bf16[39,512]{1,0:T(8,128)(2,1)S(1)} copy-done((bf16[39,512]{1,0:T(8,128)(2,1)S(1)}, bf16[39,512]{1,0:T(8,128)(2,1)}, u32[]{:S(2)}) %copy-start) | copy-done | bytes 39960
  9.5 1.8 %tables.1 = (bf16[128,1536]{1,0:T(8,128)(2,1)S(1)}, bf16[128,512]{1,0:T(8,128)(2,1)S(1)}) custom-call(bf16[39,512]{1,0:T(8,128)(2,1)S(1)} %copy-done, bf16[2,512,1536]{2,1,0:T(8,128)(2,1)} %wq_hbm.3), custom_call_target="tpu_custom_call" | custom-call | tf_op jit(solution)/shard_map/tables/pallas_call | solution.py:463
  11.3 3.9 %all-to-all-done.ids_ref = s32[16,4,128]{2,1,0:T(4,128)S(1)} async-done(((s32[16,4,128]{2,1,0:T(4,128)}), s32[16,4,128]{2,1,0:T(4,128)S(1)}, u32[]{:S(2)}, u32[]{:S(2)}) %all-to-all-start) | async-done | bytes 32800 | tf_op jit(solution)/shard_map/all_to_all | solution.py:461
  15.2 7.1 %first.1 = (bf16[768,512]{1,0:T(8,128)(2,1)S(1)}, bf16[512,1536]{1,0:T(8,128)(2,1)S(1)}, bf16[512,512]{1,0:T(8,128)(2,1)S(1)}, bf16[3,3,512,256]{3,2,1,0:T(8,128)(2,1)S(1)}) custom-call(f32[2,8]{1,0:T(2,128)} %scale_hbm.3, s32[16,4,128]{2,1,0:T(4,128)S(1)} %all-to-all-done.ids_ref, bf16[128,1536]{1,0:T(8,128)(2,1)S(1)} %get-tuple-element.15.table_ref, ...), custom_call_target="tpu_custom_call" | custom-call | tf_op jit(solution)/shard_map/first/pallas_call | solution.py:480
  22.3 0.2 collective-permute-start
  22.5 1.3 %own_keys.1 = (bf16[1536,512]{1,0:T(8,128)(2,1)S(1)}, bf16[1536,512]{1,0:T(8,128)(2,1)S(1)}, bf16[1536,512]{1,0:T(8,128)(2,1)S(1)}) custom-call(bf16[768,512]{1,0:T(8,128)(2,1)S(1)} %get-tuple-element.17.own_ref, bf16[512,1536]{1,0:T(8,128)(2,1)S(1)} %get-tuple-element.18.wq), custom_call_target="tpu_custom_call" | custom-call | tf_op jit(solution)/shard_map/own_keys/pallas_call | solution.py:516
  23.8 0.8 %collective-permute-done.other_ref = bf16[768,512]{1,0:T(8,128)(2,1)S(1)} collective-permute-done((bf16[768,512]{1,0:T(8,128)(2,1)S(1)}, bf16[768,512]{1,0:T(8,128)(2,1)S(1)}, u32[]{:S(2)}, u32[]{:S(2)}) %collective-permute-start) | collective-permute-done | bytes 786464 | tf_op jit(solution)/shard_map/ppermute | solution.py:510
  24.7 8.8 %second.1 = (bf16[8,16,256]{2,1,0:T(8,128)(2,1)}, bf16[1536,512]{1,0:T(8,128)(2,1)S(1)}, bf16[1536,512]{1,0:T(8,128)(2,1)S(1)}, bf16[1536,512]{1,0:T(8,128)(2,1)S(1)}) custom-call(f32[2,8]{1,0:T(2,128)} %scale_hbm.3, s32[16,4,128]{2,1,0:T(4,128)S(1)} %all-to-all-done.ids_ref, ...), custom_call_target="tpu_custom_call", output_to_operand_aliasing={{1}: (6, {}), {2}: (7, {}), {3}: (8, {})} | custom-call | tf_op jit(solution)/shard_map/second/pallas_call | solution.py:524
Async XLA Ops:
  1.3 13.9 %all-to-all-start = ((s32[16,4,128]{2,1,0:T(4,128)}), s32[16,4,128]{2,1,0:T(4,128)S(1)}, u32[]{:S(2)}, u32[]{:S(2)}) async-start(s32[16,4,128]{2,1,0:T(4,128)} %pad.12), calls=%async_computation | async-start | bytes 65536 | tf_op jit(solution)/shard_map/all_to_all | solution.py:461
  8.7 0.8 %copy-start = (bf16[39,512]{1,0:T(8,128)(2,1)S(1)}, bf16[39,512]{1,0:T(8,128)(2,1)}, u32[]{:S(2)}) copy-start(bf16[39,512]{1,0:T(8,128)(2,1)} %book_ref.1) | copy-start | bytes 119812
  22.3 2.4 %collective-permute-start = (bf16[768,512]{1,0:T(8,128)(2,1)S(1)}, bf16[768,512]{1,0:T(8,128)(2,1)S(1)}, u32[]{:S(2)}, u32[]{:S(2)}) collective-permute-start(bf16[768,512]{1,0:T(8,128)(2,1)S(1)} %get-tuple-element.17.own_ref), channel_id=1, source_target_pairs={{0,4},{4,0},{8,12},{12,8},{1,5},{5,1},{9,13},{13,9},{2,6},{6,2},{1... | collective-permute-start | bytes 2359304 | tf_op jit(solution)/shard_map/ppermute | solution.py:510

commit v5 on v4

--- a/solution.py
+++ b/solution.py
@@ -143,10 +143,10 @@
     return pl.ds(pl.multiple_of(tile * AREA, AREA), count)
 
 
-def neighbours(geo, lists_ref, gi, gj, row0, col0, cols):
+def neighbours(geo, lists_ref, gi, gj, row0, col0, cols, skipped=0):
     gi = jnp.clip(gi, 0, geo.tr - 1)
     gj = jnp.clip(gj, 0, geo.tc - 1)
-    owner = gi // geo.qr * (geo.tc // geo.qc) + gj // geo.qc
+    owner = gi // geo.qr * (geo.tc // geo.qc) + gj // geo.qc - skipped
     at = gi % geo.qr * geo.qc + gj % geo.qc
     bias_tile = lax.broadcasted_iota(i32, (1, NSEL * AREA), 1) // AREA
     starts = []
@@ -329,13 +329,38 @@
 
 
 STRIP = 16
-
-
-def second_body(
+EARLY = 2
+
+
+def finish(queries, attended, wo, inside):
+    h = (queries.astype(f32) + mm(attended, wo)).astype(bf16).astype(f32)
+    v = h * lax.rsqrt(square_mean(h) + norm_eps)
+    act = v / (1.0 + jnp.exp(-v))
+    share = act.shape[0] // len(inside)
+    return [
+        jnp.where(flag, act[share * n : share * n + share], 0.0) for n, flag in enumerate(inside)
+    ]
+
+
+def on_grid(geo, gi, gj):
+    return (gi >= 0) & (gi < geo.tr) & (gj >= 0) & (gj < geo.tc)
+
+
+def strip_tiles(geo, own_r, own_c, side):
+    above = (own_r - 1, AREA - STRIP)
+    below = (own_r + geo.qr, 0)
+    if geo.sides == 2:
+        edges = [tuple(jnp.where(side == 0, x, y) for x, y in zip(above, below))]
+    else:
+        edges = [above, below]
+    return [(gi, own_c - 1 + j, skip) for gi, skip in edges for j in range(geo.qc + 2)]
+
+
+def rows_body(
     geo,
-    scale_hbm, ids_ref, other_ref, wq, wo, wc, hid_in, k1_in, v1_in,
-    out_ref, hid, k1, v1,
-    lists_ref, scale_ref, queries, q1, att, region, sems,
+    scale_hbm, ids_ref, other_ref, wq, wo, hid_in, k1_in, v1_in,
+    middle, edge, queries_out, q1_out, early, hid, k1, v1,
+    lists_ref, scale_ref, queries, q1, att, sems,
 ):
     copies = [
         pltpu.make_async_copy(ids_ref.at[:, pl.ds(geo.rr, geo.qr * geo.qc), :], lists_ref, sems.at[0]),
@@ -358,8 +383,7 @@
         return (ci - p0) * c0n + cj - c0
 
     whole = [(own_r + i, own_c - 1 + j) for i in range(qr) for j in range(ring)]
-    strips = [(own_r - 1, own_c - 1 + j, AREA - STRIP) for j in range(ring)]
-    strips += [(own_r + qr, own_c - 1 + j, 0) for j in range(ring)]
+    strips = strip_tiles(geo, own_r, own_c, side)
     base = len(whole) * AREA
     for n, (gi, gj) in enumerate(whole):
         queries[AREA * n : AREA * n + AREA, :] = hid[rows_at(clipped(gi, gj)), :]
@@ -369,7 +393,10 @@
         queries[at : at + STRIP, :] = hid[here, :]
     h = queries[...]
     ms = square_mean(h.astype(f32)) + norm_eps
-    q1[...] = head_scale(mm(h, wq[:, :D]), ones_bd, norm_eps * ms)
+    q = head_scale(mm(h, wq[:, :D]), ones_bd, norm_eps * ms)
+    q1[...] = q[:base]
+    q1_out[...] = q[base:]
+    queries_out[...] = h[base:]
 
     for copy in copies:
         copy.wait()
@@ -378,35 +405,79 @@
         starts, bias = neighbours(geo, lists_ref, gi, gj, p0, c0, c0n)
         at = slice(AREA * n, AREA * n + AREA)
         att[at, :] = attend_tile(q1[at, :], starts, bias, factors, k1, v1, lane_head)
+    for n, (gi, gj, _) in enumerate(strips[:EARLY]):
+        starts, bias = neighbours(geo, lists_ref, gi, gj, p0, c0, c0n)
+        at = slice(STRIP * n, STRIP * n + STRIP)
+        early[at, :] = attend_strip(q[base:][at], starts, bias, factors, k1, v1)
+
+    done = finish(
+        queries[:base, :], att[...], wo[...], [on_grid(geo, gi, gj) for gi, gj in whole]
+    )
+    for n, tile in enumerate(done):
+        i, j = divmod(n, ring)
+        for r in range(TILE):
+            middle[TILE * i + r, TILE * j : TILE * j + TILE, :] = tile[TILE * r : TILE * r + TILE]
+    for j in range(ring):
+        last = done[(qr - 1) * ring + j][AREA - TILE :]
+        edge[TILE * j : TILE * j + TILE, :] = jnp.where(side == 0, last, done[j][:TILE]).astype(bf16)
+
+
+def rim_body(
+    geo,
+    scale_vmem, ids_ref, queries, q1, early, k1, v1, wo,
+    outer,
+    lists_ref, scale_ref, att, sems,
+):
+    own_r, own_c, side, p0, r0, c0, r1, c1 = geo.place()
+    strips = strip_tiles(geo, own_r, own_c, side)
+    owners = lists_ref.shape[0]
+    skipped = 0
+    if geo.sides == 2:
+        skipped = jnp.clip(strips[0][0], 0, geo.tr - 1) // geo.qr * owners
+    copies = [
+        pltpu.make_async_copy(
+            ids_ref.at[pl.ds(skipped, owners), pl.ds(geo.rr, geo.qr * geo.qc), :],
+            lists_ref,
+            sems.at[0],
+        ),
+        pltpu.make_async_copy(scale_vmem, scale_ref, sems.at[1]),
+    ]
+    for copy in copies:
+        copy.start()
+    for copy in copies:
+        copy.wait()
+    factors = factors_of(scale_ref, 1)
+    att[: STRIP * EARLY, :] = early[...]
     for n, (gi, gj, _) in enumerate(strips):
-        starts, bias = neighbours(geo, lists_ref, gi, gj, p0, c0, c0n)
-        at = slice(base + STRIP * n, base + STRIP * n + STRIP)
+        if n < EARLY:
+            continue
+        starts, bias = neighbours(geo, lists_ref, gi, gj, p0, c0, geo.c0n, skipped)
+        at = slice(STRIP * n, STRIP * n + STRIP)
         att[at, :] = attend_strip(q1[at, :], starts, bias, factors, k1, v1)
-
-    h = (queries[...].astype(f32) + mm(att[...], wo[...])).astype(bf16).astype(f32)
-    v = h * lax.rsqrt(square_mean(h) + norm_eps)
-    act = v / (1.0 + jnp.exp(-v))
-
-    def kept(piece, gi, gj):
-        inside = (gi >= 0) & (gi < geo.tr) & (gj >= 0) & (gj < geo.tc)
-        return jnp.where(inside, piece, 0.0)
-
-    for n, (gi, gj) in enumerate(whole):
-        i, j = divmod(n, ring)
-        tile = kept(act[AREA * n : AREA * n + AREA], gi, gj)
-        for r in range(TILE):
-            region[1 + TILE * i + r, TILE * j : TILE * j + TILE, :] = tile[TILE * r : TILE * r + TILE]
-    for n, (gi, gj, skip) in enumerate(strips):
-        i, j = divmod(n, ring)
-        at = base + STRIP * n + (STRIP - TILE if skip else 0)
-        row = (qr * TILE + 1) * i
-        region[row, TILE * j : TILE * j + TILE, :] = kept(act[at : at + TILE], gi, gj)
-
-    rows, cols = qr * TILE, qc * TILE
+    done = finish(
+        queries[...], att[...], wo[...], [on_grid(geo, gi, gj) for gi, gj, _ in strips]
+    )
+    for n, (strip, (_, _, skip)) in enumerate(zip(done, strips)):
+        row = jnp.where(skip > 0, strip[STRIP - TILE :], strip[:TILE])
+        outer[TILE * n : TILE * n + TILE, :] = row.astype(bf16)
+
+
+def conv_body(geo, middle, outer, received, wc, out_ref, region):
+    rows, cols = geo.qr * TILE, geo.qc * TILE
+    side = geo.place()[2]
+    wide = (geo.qc + 2) * TILE
+    first = outer[:wide, :].astype(f32)
+    second = (received if geo.sides == 2 else outer)[-wide:, :].astype(f32)
+    if geo.sides == 2:
+        first, second = jnp.where(side == 0, first, second), jnp.where(side == 0, second, first)
+    region[0] = first
+    region[1] = second
     total = jnp.zeros((rows * cols, wc.shape[-1]), f32)
     for dc in range(3):
         left = TILE - 1 + dc
-        shifted = region[:, left : left + cols, :].astype(bf16)
+        inner = middle[:, left : left + cols, :].astype(bf16)
+        rims = region[:, left : left + cols, :].astype(bf16)
+        shifted = jnp.concatenate([rims[:1], inner, rims[1:]], axis=0)
         for dr in range(3):
             piece = shifted[dr : dr + rows].reshape(rows * cols, D)
             total = total + mm(piece, wc[dr, dc])
@@ -510,37 +581,70 @@
         other = lax.ppermute(own, "ha", [(n, n ^ 1) for n in range(down)])
 
     n0 = geo.r0n * geo.c0n * AREA
-    nq = qr * (qc + 2) * AREA + 2 * (qc + 2) * STRIP
+    ring = qc + 2
+    whole = qr * ring * AREA
+    strips = ring * STRIP * (3 - geo.sides)
     window = pltpu.VMEM((n0, D), bf16)
     wq1, wo1, wc = map(on_chip, (wq1, wo1, wc))
+    limit = pltpu.CompilerParams(vmem_limit_bytes=VMEM_LIMIT)
+    scale, everyone = off_chip(logit_scale), on_chip(everyone)
     state = pl.pallas_call(
         functools.partial(own_keys_body, geo),
         out_shape=(window,) * 3,
         in_specs=[vmem, vmem],
         out_specs=(vmem,) * 3,
-        compiler_params=pltpu.CompilerParams(vmem_limit_bytes=VMEM_LIMIT),
+        compiler_params=limit,
         name="own_keys",
     )(on_chip(own), wq1)
-    return pl.pallas_call(
-        functools.partial(second_body, geo),
-        out_shape=(jax.ShapeDtypeStruct((qr * TILE, qc * TILE, cout), bf16),) + (window,) * 3,
-        in_specs=[hbm] + [vmem] * 8,
-        out_specs=(vmem,) * 4,
-        input_output_aliases={6: 1, 7: 2, 8: 3},
+    middle, edge, queries, q1, early, _, k1, v1 = pl.pallas_call(
+        functools.partial(rows_body, geo),
+        out_shape=(
+            pltpu.VMEM((qr * TILE, ring * TILE, D), f32),
+            pltpu.VMEM((ring * TILE, D), bf16),
+            pltpu.VMEM((strips, D), bf16),
+            pltpu.VMEM((strips, D), bf16),
+            pltpu.VMEM((STRIP * EARLY, D), bf16),
+        )
+        + (window,) * 3,
+        in_specs=[hbm] + [vmem] * 7,
+        out_specs=(vmem,) * 8,
+        input_output_aliases={5: 5, 6: 6, 7: 7},
         scratch_shapes=[
             *scalars,
-            pltpu.VMEM((nq, D), bf16),
-            pltpu.VMEM((nq, D), bf16),
-            pltpu.VMEM((nq, D), bf16),
-            pltpu.VMEM((qr * TILE + 2, (qc + 2) * TILE, D), f32),
+            pltpu.VMEM((whole + strips, D), bf16),
+            pltpu.VMEM((whole, D), bf16),
+            pltpu.VMEM((whole, D), bf16),
             pltpu.SemaphoreType.DMA((2,)),
         ],
-        compiler_params=pltpu.CompilerParams(vmem_limit_bytes=VMEM_LIMIT),
-        name="second",
-    )(
-        off_chip(logit_scale), on_chip(everyone), on_chip(other), wq1, wo1, wc,
-        *map(on_chip, state),
-    )[0]
+        compiler_params=limit,
+        name="rows",
+    )(scale, everyone, on_chip(other), wq1, wo1, *map(on_chip, state))
+    received = edge
+    if geo.sides == 2:
+        received = lax.ppermute(edge, "ha", [(n, n ^ 1) for n in range(down)])
+    outer = pl.pallas_call(
+        functools.partial(rim_body, geo),
+        out_shape=pltpu.VMEM((ring * TILE * (3 - geo.sides), D), bf16),
+        in_specs=[vmem] * 8,
+        out_specs=vmem,
+        scratch_shapes=[
+            pltpu.SMEM((across if geo.sides == 2 else down * across, qr * qc, lanes), i32),
+            scalars[1],
+            pltpu.VMEM((strips, D), bf16),
+            pltpu.SemaphoreType.DMA((2,)),
+        ],
+        compiler_params=limit,
+        name="rim",
+    )(on_chip(logit_scale), everyone, *map(on_chip, (queries, q1, early, k1, v1)), wo1)
+    return pl.pallas_call(
+        functools.partial(conv_body, geo),
+        out_shape=jax.ShapeDtypeStruct((qr * TILE, qc * TILE, cout), bf16),
+        in_specs=[vmem] * 4,
+        out_specs=vmem,
+        scratch_shapes=[pltpu.VMEM((2, ring * TILE, D), f32)],
+        compiler_params=limit,
+        name="conv",
+    )(*map(on_chip, (middle, outer, received)), wc)
 
 
 def solution(mesh):

time: 33.9 us -> 32.9 us (0.971)
  Pallas kernels: 19.1 us -> 18 us
    pallas_call x1 -> x3, Pallas kernels: 8.83 us -> 7.76 us  [the longest x1 4.74 us: local(): pl.pallas_call(functools.partial(rows_body, geo), out_shape=(pltpu.VMEM((...]
    unnamed x2 -> x4, local copies, waits for them, and re-layouts: 0.77 us -> 0.78 us
  transfers between devices with their start and end apart: 2 -> 3, of which waited for: 2 -> 2; matrix products, arithmetic and copies ran while one was open for 0% -> 0% of each run, Pallas kernels for 9% -> 15%
where the time goes in v5:
time: 32.9 us; the launch traced here: 32.7 us
  Pallas kernels  18 us (55%)
  starting transfers between devices  7.78 us (24%)
  waiting for transfers between devices  4.74 us (14%)
  local copies, waits for them, and re-layouts  1.4 us (4%)
  other arithmetic  0.7 us (2%)
    all_to_all x1, starting transfers between devices, local(): everyone = lax.all_to_all(mine, ('ha', 'wa'), 0, 0, tiled=True)  7.39 us
    pallas_call x1, Pallas kernels, local(): pl.pallas_call(functools.partial(first_body, geo), out_shape=(pltpu.VMEM(...  7.09 us
    pallas_call x1, Pallas kernels, local(): pl.pallas_call(functools.partial(rows_body, geo), out_shape=(pltpu.VMEM((...  4.74 us
    all_to_all x1, waiting for transfers between devices, local(): everyone = lax.all_to_all(mine, ('ha', 'wa'), 0, 0, tiled=True)  3.9 us
    pallas_call x1, Pallas kernels, local(): pl.pallas_call(functools.partial(rim_body, geo), out_shape=pltpu.VMEM((ri...  1.89 us
    pallas_call x1, Pallas kernels, local(): pl.pallas_call(table_body, out_shape=(pltpu.VMEM((128, 3 * D), bf16), plt...  1.81 us
    pallas_call x1, Pallas kernels, local(): pl.pallas_call(functools.partial(own_keys_body, geo), out_shape=(window,)...  1.33 us
    pallas_call x1, Pallas kernels, local(): pl.pallas_call(functools.partial(conv_body, geo), out_shape=jax.ShapeDtyp...  1.13 us
  transfers between devices with their start and end apart: 3, of which 2 were waited for; matrix products, arithmetic and copies ran while one was open for 0% of the time, Pallas kernels for 15%

profile of v5, /device:TPU:0, one launch (start us, length us, event | category | flops | bytes accessed | tf_op | source)
XLA Modules:
  0.0 32.7 jit_solution(13888726034004315469)
XLA Ops:
  0.0 0.7 %pad_add_fusion = s32[4,128]{1,0:T(4,128)S(1)} fusion(s32[2,6]{1,0:T(2,128)} %bitcast.1, s32[2,64]{1,0:T(2,128)} %param.7), kind=kLoop, calls=%fused_computation | loop fusion | flops 512 | bytes 2608 | tf_op jit(solution)/shard_map/add | solution.py:527
  0.7 0.6 %pad.12 = s32[16,4,128]{2,1,0:T(4,128)} broadcast(s32[4,128]{1,0:T(4,128)S(1)} %pad_add_fusion), dimensions={1,2} | broadcast | bytes 34816 | tf_op jit(solution)/shard_map/jit(_pad)/pad | solution.py:527
  1.3 7.4 %all-to-all-start = ((s32[16,4,128]{2,1,0:T(4,128)}), s32[16,4,128]{2,1,0:T(4,128)S(1)}, u32[]{:S(2)}, u32[]{:S(2)}) async-start(s32[16,4,128]{2,1,0:T(4,128)} %pad.12), calls=%async_computation | async-start | bytes 65536 | tf_op jit(solution)/shard_map/all_to_all | solution.py:532
  8.7 0.0 copy-start
  8.7 0.8 %copy-done = bf16[39,512]{1,0:T(8,128)(2,1)S(1)} copy-done((bf16[39,512]{1,0:T(8,128)(2,1)S(1)}, bf16[39,512]{1,0:T(8,128)(2,1)}, u32[]{:S(2)}) %copy-start) | copy-done | bytes 39960
  9.5 1.8 %tables.1 = (bf16[128,1536]{1,0:T(8,128)(2,1)S(1)}, bf16[128,512]{1,0:T(8,128)(2,1)S(1)}) custom-call(bf16[39,512]{1,0:T(8,128)(2,1)S(1)} %copy-done, bf16[2,512,1536]{2,1,0:T(8,128)(2,1)} %wq_hbm.3), custom_call_target="tpu_custom_call" | custom-call | tf_op jit(solution)/shard_map/tables/pallas_call | solution.py:534
  11.3 3.9 %all-to-all-done.ids_ref = s32[16,4,128]{2,1,0:T(4,128)S(1)} async-done(((s32[16,4,128]{2,1,0:T(4,128)}), s32[16,4,128]{2,1,0:T(4,128)S(1)}, u32[]{:S(2)}, u32[]{:S(2)}) %all-to-all-start) | async-done | bytes 32800 | tf_op jit(solution)/shard_map/all_to_all | solution.py:532
  15.2 7.1 %first.1 = (bf16[768,512]{1,0:T(8,128)(2,1)S(1)}, bf16[512,1536]{1,0:T(8,128)(2,1)S(1)}, bf16[512,512]{1,0:T(8,128)(2,1)S(1)}, bf16[3,3,512,256]{3,2,1,0:T(8,128)(2,1)S(1)}) custom-call(f32[2,8]{1,0:T(2,128)} %scale_vmem.1, s32[16,4,128]{2,1,0:T(4,128)S(1)} %all-to-all-done.ids_ref, bf16[128,1536]{1,0:T(8,128)(2,1)S(1)} %get-tuple-element.21.table_ref, ...), custom_call_target="tpu_custom_call" | custom-call | tf_op jit(solution)/shard_map/first/pallas_call | solution.py:551
  22.3 0.2 collective-permute-start
  22.5 1.3 %own_keys.1 = (bf16[1536,512]{1,0:T(8,128)(2,1)S(1)}, bf16[1536,512]{1,0:T(8,128)(2,1)S(1)}, bf16[1536,512]{1,0:T(8,128)(2,1)S(1)}) custom-call(bf16[768,512]{1,0:T(8,128)(2,1)S(1)} %get-tuple-element.23.own_ref, bf16[512,1536]{1,0:T(8,128)(2,1)S(1)} %get-tuple-element.24.wq), custom_call_target="tpu_custom_call" | custom-call | tf_op jit(solution)/shard_map/own_keys/pallas_call | solution.py:591
  23.8 0.8 %collective-permute-done.other_ref = bf16[768,512]{1,0:T(8,128)(2,1)S(1)} collective-permute-done((bf16[768,512]{1,0:T(8,128)(2,1)S(1)}, bf16[768,512]{1,0:T(8,128)(2,1)S(1)}, u32[]{:S(2)}, u32[]{:S(2)}) %collective-permute-start) | collective-permute-done | bytes 786464 | tf_op jit(solution)/shard_map/ppermute | solution.py:581
  24.7 0.0 copy-start.1
  24.7 4.7 %rows.1 = (f32[8,32,512]{2,1,0:T(8,128)S(1)}, bf16[32,512]{1,0:T(8,128)(2,1)S(1)}, bf16[64,512]{1,0:T(8,128)(2,1)S(1)}, bf16[64,512]{1,0:T(8,128)(2,1)S(1)}, bf1...) custom-call(f32[2,8]{1,0:T(2,128)} %scale_vmem.1, ...), custom_call_target="tpu_custom_call", output_to_operand_aliasing={{5}: (5, {}), {6}: (6, {}), {7}: (7, {})} | custom-call | tf_op jit(solution)/shard_map/rows/pallas_call | solution.py:599
  29.4 0.2 collective-permute-start.1
  29.6 0.0 copy-done.1
  29.6 1.9 %rim.1.outer = bf16[32,512]{1,0:T(8,128)(2,1)S(1)} custom-call(f32[2,8]{1,0:T(2,128)S(1)} %copy-done.1, s32[16,4,128]{2,1,0:T(4,128)S(1)} %all-to-all-done.ids_ref, bf16[64,512]{1,0:T(8,128)(2,1)S(1)} %get-tuple-element.30.queries, bf16[64,512]{1,0:T(8,128)(2,1)S(1)} %get-tuple-element.31.q1, bf16[32,512]{1,0:T(8,128)(2,1)S(1)} %get-tuple-element.32.early, ...), custom_call_target="tpu_custom_call" | custom-call | tf_op jit(solution)/shard_map/rim/pallas_call | solution.py:625
  31.5 0.0 collective-permute-done.1.received
  31.5 1.1 %conv.1 = bf16[8,16,256]{2,1,0:T(8,128)(2,1)} custom-call(f32[8,32,512]{2,1,0:T(8,128)S(1)} %get-tuple-element.29.middle, bf16[32,512]{1,0:T(8,128)(2,1)S(1)} %rim.1.outer, bf16[32,512]{1,0:T(8,128)(2,1)S(1)} %collective-permute-done.1.received, bf16[3,3,512,256]{3,2,1,0:T(8,128)(2,1)S(1)} %get-tuple-element.36.wc), custom_call_target="tpu_custom_call" | custom-call | tf_op jit(solution)/shard_map/conv/pallas_call | solution.py:639
Async XLA Ops:
  1.3 13.9 %all-to-all-start = ((s32[16,4,128]{2,1,0:T(4,128)}), s32[16,4,128]{2,1,0:T(4,128)S(1)}, u32[]{:S(2)}, u32[]{:S(2)}) async-start(s32[16,4,128]{2,1,0:T(4,128)} %pad.12), calls=%async_computation | async-start | bytes 65536 | tf_op jit(solution)/shard_map/all_to_all | solution.py:532
  8.7 0.8 %copy-start = (bf16[39,512]{1,0:T(8,128)(2,1)S(1)}, bf16[39,512]{1,0:T(8,128)(2,1)}, u32[]{:S(2)}) copy-start(bf16[39,512]{1,0:T(8,128)(2,1)} %book_ref.1) | copy-start | bytes 119812
  22.3 2.4 %collective-permute-start = (bf16[768,512]{1,0:T(8,128)(2,1)S(1)}, bf16[768,512]{1,0:T(8,128)(2,1)S(1)}, u32[]{:S(2)}, u32[]{:S(2)}) collective-permute-start(bf16[768,512]{1,0:T(8,128)(2,1)S(1)} %get-tuple-element.23.own_ref), channel_id=1, source_target_pairs={{0,4},{4,0},{8,12},{12,8},{1,5},{5,1},{9,13},{13,9},{2,6},{6,2},{1... | collective-permute-start | bytes 2359304 | tf_op jit(solution)/shard_map/ppermute | solution.py:581
  24.7 5.0 %copy-start.1 = (f32[2,8]{1,0:T(2,128)S(1)}, f32[2,8]{1,0:T(2,128)}, u32[]{:S(2)}) copy-start(f32[2,8]{1,0:T(2,128)} %scale_vmem.1) | copy-start | bytes 196
  29.4 2.1 %collective-permute-start.1 = (bf16[32,512]{1,0:T(8,128)(2,1)S(1)}, bf16[32,512]{1,0:T(8,128)(2,1)S(1)}, u32[]{:S(2)}, u32[]{:S(2)}) collective-permute-start(bf16[32,512]{1,0:T(8,128)(2,1)S(1)} %get-tuple-element.35), channel_id=1, source_target_pairs={{0,4},{4,0},{8,12},{12,8},{1,5},{5,1},{9,13},{13,9},{2,6},{6,2},{1... | collective-permute-start | bytes 98312 | tf_op jit(solution)/shard_map/ppermute | solution.py:624

commit v6 on v5

--- a/solution.py
+++ b/solution.py
@@ -329,7 +329,6 @@
 
 
 STRIP = 16
-EARLY = 2
 
 
 def finish(queries, attended, wo, inside):
@@ -359,8 +358,8 @@
 def rows_body(
     geo,
     scale_hbm, ids_ref, other_ref, wq, wo, hid_in, k1_in, v1_in,
-    middle, edge, queries_out, q1_out, early, hid, k1, v1,
-    lists_ref, scale_ref, queries, q1, att, sems,
+    edge, queries, att, hid, k1, v1,
+    lists_ref, scale_ref, q1, sems,
 ):
     copies = [
         pltpu.make_async_copy(ids_ref.at[:, pl.ds(geo.rr, geo.qr * geo.qc), :], lists_ref, sems.at[0]),
@@ -394,9 +393,7 @@
     h = queries[...]
     ms = square_mean(h.astype(f32)) + norm_eps
     q = head_scale(mm(h, wq[:, :D]), ones_bd, norm_eps * ms)
-    q1[...] = q[:base]
-    q1_out[...] = q[base:]
-    queries_out[...] = h[base:]
+    q1[...] = q
 
     for copy in copies:
         copy.wait()
@@ -405,59 +402,46 @@
         starts, bias = neighbours(geo, lists_ref, gi, gj, p0, c0, c0n)
         at = slice(AREA * n, AREA * n + AREA)
         att[at, :] = attend_tile(q1[at, :], starts, bias, factors, k1, v1, lane_head)
-    for n, (gi, gj, _) in enumerate(strips[:EARLY]):
+    for n, (gi, gj, _) in enumerate(strips):
         starts, bias = neighbours(geo, lists_ref, gi, gj, p0, c0, c0n)
-        at = slice(STRIP * n, STRIP * n + STRIP)
-        early[at, :] = attend_strip(q[base:][at], starts, bias, factors, k1, v1)
-
+        at = slice(base + STRIP * n, base + STRIP * n + STRIP)
+        att[at, :] = attend_strip(q1[at, :], starts, bias, factors, k1, v1)
+
+    picked = [
+        pl.ds(
+            pl.multiple_of(
+                jnp.where(side == 0, ((qr - 1) * ring + j) * AREA + AREA - STRIP, j * AREA), STRIP
+            ),
+            STRIP,
+        )
+        for j in range(ring)
+    ]
     done = finish(
-        queries[:base, :], att[...], wo[...], [on_grid(geo, gi, gj) for gi, gj in whole]
+        jnp.concatenate([queries[at, :] for at in picked], axis=0),
+        jnp.concatenate([att[at, :] for at in picked], axis=0),
+        wo[...],
+        [on_grid(geo, own_r, own_c - 1 + j) for j in range(ring)],
     )
-    for n, tile in enumerate(done):
-        i, j = divmod(n, ring)
-        for r in range(TILE):
-            middle[TILE * i + r, TILE * j : TILE * j + TILE, :] = tile[TILE * r : TILE * r + TILE]
-    for j in range(ring):
-        last = done[(qr - 1) * ring + j][AREA - TILE :]
-        edge[TILE * j : TILE * j + TILE, :] = jnp.where(side == 0, last, done[j][:TILE]).astype(bf16)
-
-
-def rim_body(
-    geo,
-    scale_vmem, ids_ref, queries, q1, early, k1, v1, wo,
-    outer,
-    lists_ref, scale_ref, att, sems,
-):
-    own_r, own_c, side, p0, r0, c0, r1, c1 = geo.place()
+    for j, strip in enumerate(done):
+        row = jnp.where(side == 0, strip[STRIP - TILE :], strip[:TILE])
+        edge[TILE * j : TILE * j + TILE, :] = row.astype(bf16)
+
+
+def finish_body(geo, queries, att, wo, middle, outer):
+    own_r, own_c, side = geo.place()[:3]
+    qr, ring = geo.qr, geo.qc + 2
+    whole = [(own_r + i, own_c - 1 + j) for i in range(qr) for j in range(ring)]
     strips = strip_tiles(geo, own_r, own_c, side)
-    owners = lists_ref.shape[0]
-    skipped = 0
-    if geo.sides == 2:
-        skipped = jnp.clip(strips[0][0], 0, geo.tr - 1) // geo.qr * owners
-    copies = [
-        pltpu.make_async_copy(
-            ids_ref.at[pl.ds(skipped, owners), pl.ds(geo.rr, geo.qr * geo.qc), :],
-            lists_ref,
-            sems.at[0],
-        ),
-        pltpu.make_async_copy(scale_vmem, scale_ref, sems.at[1]),
-    ]
-    for copy in copies:
-        copy.start()
-    for copy in copies:
-        copy.wait()
-    factors = factors_of(scale_ref, 1)
-    att[: STRIP * EARLY, :] = early[...]
-    for n, (gi, gj, _) in enumerate(strips):
-        if n < EARLY:
-            continue
-        starts, bias = neighbours(geo, lists_ref, gi, gj, p0, c0, geo.c0n, skipped)
-        at = slice(STRIP * n, STRIP * n + STRIP)
-        att[at, :] = attend_strip(q1[at, :], starts, bias, factors, k1, v1)
-    done = finish(
-        queries[...], att[...], wo[...], [on_grid(geo, gi, gj) for gi, gj, _ in strips]
-    )
-    for n, (strip, (_, _, skip)) in enumerate(zip(done, strips)):
+    base = len(whole) * AREA
+    flags = [on_grid(geo, gi, gj) for gi, gj in whole for _ in range(AREA // STRIP)]
+    flags += [on_grid(geo, gi, gj) for gi, gj, _ in strips]
+    done = finish(queries[...], att[...], wo[...], flags)
+    for n, piece in enumerate(done[: base // STRIP]):
+        i, j = divmod(n // (AREA // STRIP), ring)
+        row = TILE * i + n % (AREA // STRIP) * (STRIP // TILE)
+        for r in range(STRIP // TILE):
+            middle[row + r, TILE * j : TILE * j + TILE, :] = piece[TILE * r : TILE * r + TILE]
+    for n, (strip, (_, _, skip)) in enumerate(zip(done[base // STRIP :], strips)):
         row = jnp.where(skip > 0, strip[STRIP - TILE :], strip[:TILE])
         outer[TILE * n : TILE * n + TILE, :] = row.astype(bf16)
 
@@ -596,46 +580,31 @@
         compiler_params=limit,
         name="own_keys",
     )(on_chip(own), wq1)
-    middle, edge, queries, q1, early, _, k1, v1 = pl.pallas_call(
+    pieces = pltpu.VMEM((whole + strips, D), bf16)
+    edge, queries, att = pl.pallas_call(
         functools.partial(rows_body, geo),
-        out_shape=(
-            pltpu.VMEM((qr * TILE, ring * TILE, D), f32),
-            pltpu.VMEM((ring * TILE, D), bf16),
-            pltpu.VMEM((strips, D), bf16),
-            pltpu.VMEM((strips, D), bf16),
-            pltpu.VMEM((STRIP * EARLY, D), bf16),
-        )
-        + (window,) * 3,
+        out_shape=(pltpu.VMEM((ring * TILE, D), bf16), pieces, pieces) + (window,) * 3,
         in_specs=[hbm] + [vmem] * 7,
-        out_specs=(vmem,) * 8,
-        input_output_aliases={5: 5, 6: 6, 7: 7},
-        scratch_shapes=[
-            *scalars,
-            pltpu.VMEM((whole + strips, D), bf16),
-            pltpu.VMEM((whole, D), bf16),
-            pltpu.VMEM((whole, D), bf16),
-            pltpu.SemaphoreType.DMA((2,)),
-        ],
+        out_specs=(vmem,) * 6,
+        input_output_aliases={5: 3, 6: 4, 7: 5},
+        scratch_shapes=[*scalars, pieces, pltpu.SemaphoreType.DMA((2,))],
         compiler_params=limit,
         name="rows",
-    )(scale, everyone, on_chip(other), wq1, wo1, *map(on_chip, state))
+    )(scale, everyone, on_chip(other), wq1, wo1, *map(on_chip, state))[:3]
     received = edge
     if geo.sides == 2:
         received = lax.ppermute(edge, "ha", [(n, n ^ 1) for n in range(down)])
-    outer = pl.pallas_call(
-        functools.partial(rim_body, geo),
-        out_shape=pltpu.VMEM((ring * TILE * (3 - geo.sides), D), bf16),
-        in_specs=[vmem] * 8,
-        out_specs=vmem,
-        scratch_shapes=[
-            pltpu.SMEM((across if geo.sides == 2 else down * across, qr * qc, lanes), i32),
-            scalars[1],
-            pltpu.VMEM((strips, D), bf16),
-            pltpu.SemaphoreType.DMA((2,)),
-        ],
+    middle, outer = pl.pallas_call(
+        functools.partial(finish_body, geo),
+        out_shape=(
+            pltpu.VMEM((qr * TILE, ring * TILE, D), f32),
+            pltpu.VMEM((ring * TILE * (3 - geo.sides), D), bf16),
+        ),
+        in_specs=[vmem] * 3,
+        out_specs=(vmem,) * 2,
         compiler_params=limit,
-        name="rim",
-    )(on_chip(logit_scale), everyone, *map(on_chip, (queries, q1, early, k1, v1)), wo1)
+        name="finish",
+    )(on_chip(queries), on_chip(att), wo1)
     return pl.pallas_call(
         functools.partial(conv_body, geo),
         out_shape=jax.ShapeDtypeStruct((qr * TILE, qc * TILE, cout), bf16),

time: 32.9 us -> 32.7 us (level)
  Pallas kernels: 18 us -> 17.3 us
  waiting for transfers between devices: 4.74 us -> 5.16 us
    pallas_call x1, Pallas kernels: 1.89 us -> 0.63 us  [local(): pl.pallas_call(functools.partial(finish_body, geo), out_shape=(pltpu.VMEM...]
    pallas_call x1, Pallas kernels: 4.74 us -> 5.33 us  [local(): pl.pallas_call(functools.partial(rows_body, geo), out_shape=(pltpu.VMEM((...]
    ppermute x1, waiting for transfers between devices: 0.01 us -> 0.43 us  [local(): received = lax.ppermute(edge, 'ha', [(n, n ^ 1) for n in range(down)])]
    unnamed x4 -> x2, local copies, waits for them, and re-layouts: 0.78 us -> 0.77 us
  transfers between devices with their start and end apart: 3 -> 3, of which waited for: 2 -> 3; matrix products, arithmetic and copies ran while one was open for 0% -> 0% of each run, Pallas kernels for 15% -> 12%
where the time goes in v6:
time: 32.7 us; the launch traced here: 32.4 us
  Pallas kernels  17.3 us (53%)
  starting transfers between devices  7.78 us (24%)
  waiting for transfers between devices  5.16 us (16%)
  local copies, waits for them, and re-layouts  1.39 us (4%)
  other arithmetic  0.7 us (2%)
    all_to_all x1, starting transfers between devices, local(): everyone = lax.all_to_all(mine, ('ha', 'wa'), 0, 0, tiled=True)  7.39 us
    pallas_call x1, Pallas kernels, local(): pl.pallas_call(functools.partial(first_body, geo), out_shape=(pltpu.VMEM(...  7.09 us
    pallas_call x1, Pallas kernels, local(): pl.pallas_call(functools.partial(rows_body, geo), out_shape=(pltpu.VMEM((...  5.33 us
    all_to_all x1, waiting for transfers between devices, local(): everyone = lax.all_to_all(mine, ('ha', 'wa'), 0, 0, tiled=True)  3.9 us
    pallas_call x1, Pallas kernels, local(): pl.pallas_call(table_body, out_shape=(pltpu.VMEM((128, 3 * D), bf16), plt...  1.81 us
    pallas_call x1, Pallas kernels, local(): pl.pallas_call(functools.partial(own_keys_body, geo), out_shape=(window,)...  1.33 us
    pallas_call x1, Pallas kernels, local(): pl.pallas_call(functools.partial(conv_body, geo), out_shape=jax.ShapeDtyp...  1.12 us
    ppermute x1, waiting for transfers between devices, local(): other = lax.ppermute(own, 'ha', [(n, n ^ 1) for n in range(down)])  0.83 us
  transfers between devices with their start and end apart: 3, of which 3 were waited for; matrix products, arithmetic and copies ran while one was open for 0% of the time, Pallas kernels for 12%

profile of v6, /device:TPU:0, one launch (start us, length us, event | category | flops | bytes accessed | tf_op | source)
XLA Modules:
  0.0 32.4 jit_solution(1592321283508519186)
XLA Ops:
  0.0 0.7 %pad_add_fusion = s32[4,128]{1,0:T(4,128)S(1)} fusion(s32[2,6]{1,0:T(2,128)} %bitcast.1, s32[2,64]{1,0:T(2,128)} %param.7), kind=kLoop, calls=%fused_computation | loop fusion | flops 512 | bytes 2608 | tf_op jit(solution)/shard_map/add | solution.py:511
  0.7 0.6 %pad.12 = s32[16,4,128]{2,1,0:T(4,128)} broadcast(s32[4,128]{1,0:T(4,128)S(1)} %pad_add_fusion), dimensions={1,2} | broadcast | bytes 34816 | tf_op jit(solution)/shard_map/jit(_pad)/pad | solution.py:511
  1.3 7.4 %all-to-all-start = ((s32[16,4,128]{2,1,0:T(4,128)}), s32[16,4,128]{2,1,0:T(4,128)S(1)}, u32[]{:S(2)}, u32[]{:S(2)}) async-start(s32[16,4,128]{2,1,0:T(4,128)} %pad.12), calls=%async_computation | async-start | bytes 65536 | tf_op jit(solution)/shard_map/all_to_all | solution.py:516
  8.7 0.0 copy-start
  8.7 0.8 %copy-done = bf16[39,512]{1,0:T(8,128)(2,1)S(1)} copy-done((bf16[39,512]{1,0:T(8,128)(2,1)S(1)}, bf16[39,512]{1,0:T(8,128)(2,1)}, u32[]{:S(2)}) %copy-start) | copy-done | bytes 39960
  9.5 1.8 %tables.1 = (bf16[128,1536]{1,0:T(8,128)(2,1)S(1)}, bf16[128,512]{1,0:T(8,128)(2,1)S(1)}) custom-call(bf16[39,512]{1,0:T(8,128)(2,1)S(1)} %copy-done, bf16[2,512,1536]{2,1,0:T(8,128)(2,1)} %wq_hbm.3), custom_call_target="tpu_custom_call" | custom-call | tf_op jit(solution)/shard_map/tables/pallas_call | solution.py:518
  11.3 3.9 %all-to-all-done.ids_ref = s32[16,4,128]{2,1,0:T(4,128)S(1)} async-done(((s32[16,4,128]{2,1,0:T(4,128)}), s32[16,4,128]{2,1,0:T(4,128)S(1)}, u32[]{:S(2)}, u32[]{:S(2)}) %all-to-all-start) | async-done | bytes 32800 | tf_op jit(solution)/shard_map/all_to_all | solution.py:516
  15.2 7.1 %first.1 = (bf16[768,512]{1,0:T(8,128)(2,1)S(1)}, bf16[512,1536]{1,0:T(8,128)(2,1)S(1)}, bf16[512,512]{1,0:T(8,128)(2,1)S(1)}, bf16[3,3,512,256]{3,2,1,0:T(8,128)(2,1)S(1)}) custom-call(f32[2,8]{1,0:T(2,128)} %scale_hbm.3, s32[16,4,128]{2,1,0:T(4,128)S(1)} %all-to-all-done.ids_ref, bf16[128,1536]{1,0:T(8,128)(2,1)S(1)} %get-tuple-element.19.table_ref, ...), custom_call_target="tpu_custom_call" | custom-call | tf_op jit(solution)/shard_map/first/pallas_call | solution.py:535
  22.3 0.2 collective-permute-start
  22.5 1.3 %own_keys.1 = (bf16[1536,512]{1,0:T(8,128)(2,1)S(1)}, bf16[1536,512]{1,0:T(8,128)(2,1)S(1)}, bf16[1536,512]{1,0:T(8,128)(2,1)S(1)}) custom-call(bf16[768,512]{1,0:T(8,128)(2,1)S(1)} %get-tuple-element.21.own_ref, bf16[512,1536]{1,0:T(8,128)(2,1)S(1)} %get-tuple-element.22.wq), custom_call_target="tpu_custom_call" | custom-call | tf_op jit(solution)/shard_map/own_keys/pallas_call | solution.py:575
  23.8 0.8 %collective-permute-done.other_ref = bf16[768,512]{1,0:T(8,128)(2,1)S(1)} collective-permute-done((bf16[768,512]{1,0:T(8,128)(2,1)S(1)}, bf16[768,512]{1,0:T(8,128)(2,1)S(1)}, u32[]{:S(2)}, u32[]{:S(2)}) %collective-permute-start) | collective-permute-done | bytes 786464 | tf_op jit(solution)/shard_map/ppermute | solution.py:565
  24.7 5.3 %rows.1 = (bf16[32,512]{1,0:T(8,128)(2,1)S(1)}, bf16[320,512]{1,0:T(8,128)(2,1)S(1)}, bf16[320,512]{1,0:T(8,128)(2,1)S(1)}, bf16[1536,512]{1,0:T(8,128)(2,1)S(1)...) custom-call(f32[2,8]{1,0:T(2,128)} %scale_hbm.3, ...), custom_call_target="tpu_custom_call", output_to_operand_aliasing={{3}: (5, {}), {4}: (6, {}), {5}: (7, {})} | custom-call | tf_op jit(solution)/shard_map/rows/pallas_call | solution.py:584
  30.0 0.2 collective-permute-start.1
  30.2 0.6 %finish.1 = (f32[8,32,512]{2,1,0:T(8,128)S(1)}, bf16[32,512]{1,0:T(8,128)(2,1)S(1)}) custom-call(bf16[320,512]{1,0:T(8,128)(2,1)S(1)} %get-tuple-element.27.queries, bf16[320,512]{1,0:T(8,128)(2,1)S(1)} %get-tuple-element.28.att, bf16[512,512]{1,0:T(8,128)(2,1)S(1)} %get-tuple-element.23.wo), custom_call_target="tpu_custom_call" | custom-call | tf_op jit(solution)/shard_map/finish/pallas_call | solution.py:597
  30.8 0.4 %collective-permute-done.1.received = bf16[32,512]{1,0:T(8,128)(2,1)S(1)} collective-permute-done((bf16[32,512]{1,0:T(8,128)(2,1)S(1)}, bf16[32,512]{1,0:T(8,128)(2,1)S(1)}, u32[]{:S(2)}, u32[]{:S(2)}) %collective-permute-start.1) | collective-permute-done | bytes 32800 | tf_op jit(solution)/shard_map/ppermute | solution.py:596
  31.3 1.1 %conv.1 = bf16[8,16,256]{2,1,0:T(8,128)(2,1)} custom-call(f32[8,32,512]{2,1,0:T(8,128)S(1)} %get-tuple-element.29.middle, bf16[32,512]{1,0:T(8,128)(2,1)S(1)} %get-tuple-element.30.outer, bf16[32,512]{1,0:T(8,128)(2,1)S(1)} %collective-permute-done.1.received, bf16[3,3,512,256]{3,2,1,0:T(8,128)(2,1)S(1)} %get-tuple-element.32.wc), custom_call_target="tpu_custom_call" | custom-call | tf_op jit(solution)/shard_map/conv/pallas_call | solution.py:608
Async XLA Ops:
  1.3 13.9 %all-to-all-start = ((s32[16,4,128]{2,1,0:T(4,128)}), s32[16,4,128]{2,1,0:T(4,128)S(1)}, u32[]{:S(2)}, u32[]{:S(2)}) async-start(s32[16,4,128]{2,1,0:T(4,128)} %pad.12), calls=%async_computation | async-start | bytes 65536 | tf_op jit(solution)/shard_map/all_to_all | solution.py:516
  8.7 0.8 %copy-start = (bf16[39,512]{1,0:T(8,128)(2,1)S(1)}, bf16[39,512]{1,0:T(8,128)(2,1)}, u32[]{:S(2)}) copy-start(bf16[39,512]{1,0:T(8,128)(2,1)} %book_ref.1) | copy-start | bytes 119812
  22.3 2.4 %collective-permute-start = (bf16[768,512]{1,0:T(8,128)(2,1)S(1)}, bf16[768,512]{1,0:T(8,128)(2,1)S(1)}, u32[]{:S(2)}, u32[]{:S(2)}) collective-permute-start(bf16[768,512]{1,0:T(8,128)(2,1)S(1)} %get-tuple-element.21.own_ref), channel_id=1, source_target_pairs={{0,4},{4,0},{8,12},{12,8},{1,5},{5,1},{9,13},{13,9},{2,6},{6,2},{1... | collective-permute-start | bytes 2359304 | tf_op jit(solution)/shard_map/ppermute | solution.py:565
  30.0 1.3 %collective-permute-start.1 = (bf16[32,512]{1,0:T(8,128)(2,1)S(1)}, bf16[32,512]{1,0:T(8,128)(2,1)S(1)}, u32[]{:S(2)}, u32[]{:S(2)}) collective-permute-start(bf16[32,512]{1,0:T(8,128)(2,1)S(1)} %get-tuple-element.31), channel_id=1, source_target_pairs={{0,4},{4,0},{8,12},{12,8},{1,5},{5,1},{9,13},{13,9},{2,6},{6,2},{1... | collective-permute-start | bytes 98312 | tf_op jit(solution)/shard_map/ppermute | solution.py:596
